TPU v7x, 32 devices: a whole 2x2x4 slice. The times are simulated.
32 devices in a mesh: clip: 8 (over z, x), seq: 4 (over y, core).
Axes of the slice: x: 2, y: 2, z: 4, core: 2. Of those that a mesh axis runs over, the one named last changes fastest.
Arguments:
- clip_tokens: bfloat16 [8, 4, 196, 1024], P('clip', 'seq'), may hold values from -6 to 6
- attn_gain: float32 [1024], replicated, may hold values from 0.5 to 1.5
- qkv_weight: bfloat16 [1024, 3072], replicated, may hold values from -0.1875 to 0.1875
- out_weight: bfloat16 [1024, 1024], replicated, may hold values from -0.1875 to 0.1875
- head_gain: float32 [1024], replicated, may hold values from 0.5 to 1.5
- gloss_weight: bfloat16 [1024, 1200], replicated, may hold values from -1.5 to 1.5
- gloss_targets: int32 [8, 2], P('clip'), may hold values from 1 to 1199
- target_lengths: int32 [8], P('clip'), may hold values from 1 to 2, as said below
Outputs:
- clip_loss: float32 [8], P('clip')
- grad_tokens: bfloat16 [8, 4, 196, 1024], P('clip', 'seq')
- grad_attn_gain: float32 [1024], P('seq')
- grad_qkv: float32 [1024, 3072], P('seq')
- grad_out: float32 [1024, 1024], P('seq')
- grad_head_gain: float32 [1024], P('seq')
- grad_gloss: float32 [1024, 1200], P('seq')
Inputs may be any that keep to these rules, and one draw needn't show every extreme that they name: `target_lengths`: some clip has exactly 2 glosses, and some has half of 2, rounded up.
All inputs are finite; a program needn't handle non-finite values.
Results may differ from a plain program's by a relative error of at most 0.02.
Values may be sent and summed in bfloat16 or wider, within the bound.
A program may use at most 128 MiB of HBM per device.

v0:
```python
import functools

import jax
import jax.numpy as jnp
from jax import lax
from jax.experimental import pallas as pl
from jax.experimental.pallas import tpu as pltpu
from jax.sharding import PartitionSpec as P

H = 16
HD = 64
SCALE = HD ** (-0.5)

epsilon = 1e-06
very_low = -10000.0
f32 = jnp.float32
bf16 = jnp.bfloat16


def up(value, step):
    return -(-value // step) * step


def dot(left, right, dims=((1,), (0,))):
    return lax.dot_general(left, right, (dims, ((), ())), preferred_element_type=f32)


def spread(head_lanes, width, first, frame):
    row = lax.broadcasted_iota(jnp.int32, (head_lanes, width), 0)
    col = lax.broadcasted_iota(jnp.int32, (head_lanes, width), 1) + first
    return jnp.where(row == frame * H + lax.shift_right_logical(col, 6), 1.0, 0.0).astype(bf16)


def by_head(rows, head_lanes):
    count, width = rows.shape
    row = lax.broadcasted_iota(jnp.int32, (H, width), 0)
    col = lax.broadcasted_iota(jnp.int32, (H, width), 1)
    own = row == lax.shift_right_logical(col, 6)
    parts = [
        jnp.where(own, jnp.broadcast_to(rows[t : t + 1], (H, width)), 0.0) for t in range(count)
    ]
    if head_lanes > count * H:
        parts.append(jnp.zeros((head_lanes - count * H, width), f32))
    return jnp.concatenate(parts, axis=0)


def low_lanes(rows):
    return lax.broadcasted_iota(jnp.int32, (rows, 128), 1) < HD


def forward_kernel(x_ref, gain_ref, w_ref, q_ref, k_ref, v_ref, p_ref, low_ref, norm_ref, inv_ref, sum_ref):
    frames, here, width = x_ref.shape
    rows = frames * here
    head_lanes = p_ref.shape[1]
    x = x_ref[...].reshape(rows, width).astype(f32)
    centred = x - jnp.mean(x, axis=1, keepdims=True)
    inv = lax.rsqrt(jnp.mean(centred * centred, axis=1, keepdims=True) + epsilon)
    normed = centred * inv
    norm_ref[...] = normed
    inv_ref[...] = jnp.broadcast_to(inv, (rows, 128))
    low_ref[...] = (normed * gain_ref[...]).astype(bf16)
    low = low_lanes(rows)
    for pair in range(H // 2):
        y = dot(low_ref[...], w_ref[:, pair * 384 : (pair + 1) * 384])
        a, b, c = y[:, :128], y[:, 128:256], y[:, 256:]
        at = slice(pair * 128, (pair + 1) * 128)
        q_ref[:, at] = jnp.where(low, a, b).astype(bf16)
        k_ref[:, at] = pltpu.roll(jnp.where(low, c, a), HD, 1).astype(bf16)
        v_ref[:, at] = jnp.where(low, b, c).astype(bf16)
    keys = k_ref[...].astype(f32).reshape(frames, here, width)
    scores = jnp.zeros((rows, head_lanes), f32)
    for t in range(frames):
        q_t = q_ref[t * here : (t + 1) * here, :].astype(f32)
        prod = (keys * q_t[None]).reshape(rows, width).astype(bf16)
        scores += dot(prod, spread(head_lanes, width, 0, t), ((1,), (1,)))
    raised = jnp.exp(scores * SCALE).reshape(frames, here, head_lanes)
    probs = raised / jnp.sum(raised, axis=0, keepdims=True)
    probs = probs.reshape(rows, head_lanes)
    p_ref[...] = probs
    mixed = dot(probs.astype(bf16), v_ref[...], ((0,), (0,)))
    row = lax.broadcasted_iota(jnp.int32, (H, width), 0)
    col = lax.broadcasted_iota(jnp.int32, (H, width), 1)
    own = row == lax.shift_right_logical(col, 6)
    sum_ref[...] = jnp.zeros_like(sum_ref)
    for t in range(frames):
        sum_ref[0, t : t + 1, :] = jnp.sum(x[t * here : (t + 1) * here], axis=0, keepdims=True)
        sum_ref[1, t : t + 1, :] = jnp.sum(
            jnp.where(own, mixed[t * H : (t + 1) * H], 0.0), axis=0, keepdims=True
        )


def add_log(left, right):
    top = jnp.maximum(left, right)
    return top + jnp.log(1.0 + jnp.exp(-jnp.abs(left - right)))


def middle_kernel(
    patches, frames, labels_ref, length_ref, sums_ref, wo_ref, gain_ref, wg_ref,
    loss_ref, frame_ref, gl_ref, head_ref, mix_ref, low_ref, ga_ref, att_ref,
):
    total = jnp.sum(sums_ref[...], axis=0)
    sum_tok, sum_att = total[0], total[1]
    att_ref[...] = sum_att
    hi = sum_att.astype(bf16)
    lo = (sum_att - hi.astype(f32)).astype(bf16)
    pooled = (sum_tok + dot(hi, wo_ref[...]) + dot(lo, wo_ref[...])) * (1.0 / patches)
    centred = pooled - jnp.mean(pooled, axis=1, keepdims=True)
    inv = lax.rsqrt(jnp.mean(centred * centred, axis=1, keepdims=True) + epsilon)
    plain = centred * inv
    frame = (plain * gain_ref[...]).astype(bf16)
    frame_ref[...] = frame
    logits = dot(frame, wg_ref[...])
    padded, vocab = logits.shape
    raised = jnp.exp(logits)
    denom = jnp.sum(raised, axis=1, keepdims=True)
    soft = raised / denom
    logs = logits - jnp.log(denom)
    cap = labels_ref.shape[1]
    length = length_ref[0]
    lane = lax.broadcasted_iota(jnp.int32, (1, 128), 1)
    gloss = lax.broadcasted_iota(jnp.int32, (padded, vocab), 1)

    def pick(label):
        return jnp.sum(jnp.where(gloss == label, logs, 0.0), axis=1, keepdims=True)

    wide = lax.broadcasted_iota(jnp.int32, (padded, 128), 1)
    emitted = jnp.where((wide & 1) == 0, pick(0), 0.0)
    skip = lane < 0
    for i in range(cap):
        label = labels_ref[0, i]
        emitted = jnp.where(wide == 2 * i + 1, pick(label), emitted)
        before = labels_ref[0, i - 1] if i else -1
        skip = skip | ((lane == 2 * i + 1) & (label != before))
    usable = lane < 2 * length + 1
    start = (lane < 2) & usable
    alphas = jnp.where(start, emitted[0:1], very_low)
    kept = []
    for t in range(1, frames):
        one = jnp.where(lane < 1, very_low, pltpu.roll(alphas, 1, 1))
        two = jnp.where(skip, pltpu.roll(alphas, 2, 1), very_low)
        outer = add_log(add_log(alphas, one), two)
        kept.append((jnp.exp(alphas - outer), jnp.exp(one - outer), jnp.exp(two - outer)))
        alphas = jnp.where(usable, outer + emitted[t : t + 1], very_low)
    last = jnp.sum(jnp.where(lane == 2 * length, alphas, 0.0), axis=1, keepdims=True)
    prior = jnp.sum(jnp.where(lane == 2 * length - 1, alphas, 0.0), axis=1, keepdims=True)
    ending = add_log(last, prior)
    share = 1.0 / length.astype(f32)
    loss_ref[...] = jnp.broadcast_to(-ending * share, (8, 128))
    grad = jnp.where(
        (lane == 2 * length) | (lane == 2 * length - 1), -share * jnp.exp(alphas - ending), 0.0
    )
    row = lax.broadcasted_iota(jnp.int32, (padded, 128), 0)
    emit_grad = jnp.zeros((padded, 128), f32)
    for t in range(frames - 1, 0, -1):
        grad = jnp.where(usable, grad, 0.0)
        emit_grad = jnp.where(row == t, grad, emit_grad)
        w_own, w_one, w_two = kept[t - 1]
        from_one = jnp.where(lane < 1, 0.0, grad * w_one)
        from_two = jnp.where(skip, grad * w_two, 0.0)
        from_two = jnp.where(lane < 2, 0.0, from_two)
        grad = grad * w_own + pltpu.roll(from_one, 127, 1) + pltpu.roll(from_two, 126, 1)
    emit_grad = jnp.where(row == 0, jnp.where(start, grad, 0.0), emit_grad)
    blank = jnp.sum(jnp.where((wide & 1) == 0, emit_grad, 0.0), axis=1, keepdims=True)
    d_logs = jnp.where(gloss == 0, blank, 0.0)
    for i in range(cap):
        part = jnp.sum(jnp.where(wide == 2 * i + 1, emit_grad, 0.0), axis=1, keepdims=True)
        d_logs = d_logs + jnp.where(gloss == labels_ref[0, i], part, 0.0)
    d_logits = d_logs - soft * jnp.sum(emit_grad, axis=1, keepdims=True)
    gl = d_logits.astype(bf16)
    gl_ref[...] = gl
    grad_frame = dot(gl, wg_ref[...], ((1,), (1,)))
    head_ref[...] = jnp.broadcast_to(jnp.sum(grad_frame * plain, axis=0, keepdims=True), head_ref.shape)
    scaled = grad_frame * gain_ref[...]
    grad_pooled = inv * (
        scaled
        - jnp.mean(scaled, axis=1, keepdims=True)
        - plain * jnp.mean(scaled * plain, axis=1, keepdims=True)
    )
    grad_mixed = grad_pooled * (1.0 / patches)
    mix_ref[...] = grad_mixed
    mixed_low = grad_mixed.astype(bf16)
    low_ref[...] = mixed_low
    ga_ref[...] = dot(mixed_low, wo_ref[...], ((1,), (1,))).astype(bf16)


def backward_kernel(
    patches, frames, here, q_ref, k_ref, v_ref, p_ref, low_ref, norm_ref, inv_ref, ga_ref, mix_ref,
    gain_ref, w_ref, gt_ref, dw_ref, cols_ref, qk_ref,
):
    rows, width = q_ref.shape
    head_lanes = p_ref.shape[1]
    ga = by_head(ga_ref[...].astype(f32)[:frames], head_lanes).astype(bf16)
    probs = p_ref[...]
    probs_low = probs.astype(bf16)
    grad_probs = dot(v_ref[...], ga, ((1,), (1,)))
    inner = jnp.sum((grad_probs * probs).reshape(frames, here, head_lanes), axis=0, keepdims=True)
    grad_scores = probs.reshape(frames, here, head_lanes) * (
        grad_probs.reshape(frames, here, head_lanes) - inner
    )
    scores_low = (grad_scores.reshape(rows, head_lanes) * SCALE).astype(bf16)
    low = low_lanes(rows)
    for pair in range(H // 2):
        at = slice(pair * 128, (pair + 1) * 128)
        keys = k_ref[:, at].astype(f32).reshape(frames, here, 128)
        grad_keys = jnp.zeros((frames, here, 128), f32)
        queries = []
        for t in range(frames):
            wide = dot(scores_low, spread(head_lanes, 128, pair * 128, t)).reshape(frames, here, 128)
            queries.append(jnp.sum(wide * keys, axis=0))
            q_t = q_ref[t * here : (t + 1) * here, at].astype(f32)
            grad_keys += wide * q_t[None]
        gq = jnp.concatenate(queries, axis=0)
        gk = pltpu.roll(grad_keys.reshape(rows, 128), HD, 1)
        gv = dot(probs_low, ga[:, at])
        qk_ref[:, pair * 256 : pair * 256 + 128] = gq.astype(bf16)
        qk_ref[:, pair * 256 + 128 : pair * 256 + 256] = gk.astype(bf16)
        a = jnp.where(low, gq, gk).astype(bf16)
        b = jnp.where(low, gv, gq).astype(bf16)
        c = jnp.where(low, gk, gv).astype(bf16)
        part = dot(
            jnp.concatenate([a, b, c], axis=1), w_ref[:, pair * 384 : (pair + 1) * 384], ((1,), (1,))
        )
        if pair == 0:
            grad_normed = part
        else:
            grad_normed += part
    tokens_low = low_ref[...]
    chunk = 512
    for start in range(0, 2 * width, chunk):
        dw_ref[:, start : start + chunk] = dot(
            tokens_low, qk_ref[:, start : start + chunk], ((0,), (0,))
        ).astype(bf16)
    cols_ref[:, :head_lanes] = dot(tokens_low, probs_low, ((0,), (0,))).astype(bf16)
    normed = norm_ref[...]
    gain_part = (grad_normed * normed).astype(bf16)
    cols_ref[:, head_lanes:] = dot(gain_part, jnp.ones((rows, 128), bf16), ((0,), (0,))).astype(bf16)
    scaled = grad_normed * gain_ref[...]
    back = inv_ref[:, :1] * (
        scaled
        - jnp.mean(scaled, axis=1, keepdims=True)
        - normed * jnp.mean(scaled * normed, axis=1, keepdims=True)
    )
    for t in range(frames):
        gt_ref[t] = ((back[t * here : (t + 1) * here] + mix_ref[t : t + 1, :]) * patches).astype(bf16)


def final_kernel(
    frames, qk_ref, cols_ref, att_ref, mix_ref, frame_ref, gl_ref, ga_ref, head_ref,
    qkv_out, out_out, gloss_out, head_out, gain_out,
):
    clips, block, lanes = cols_ref.shape
    head_lanes = lanes - 128
    out_out[...] = dot(att_ref[...], mix_ref[...], ((0,), (0,)))
    gloss_out[...] = dot(frame_ref[...], gl_ref[...], ((0,), (0,)))
    head_out[...] = jnp.sum(head_ref[...].astype(f32), axis=0, keepdims=True)
    gain_out[...] = jnp.sum(cols_ref[:, :, head_lanes:].astype(f32), axis=0)
    values = None
    for c in range(clips):
        ga = by_head(ga_ref[c].astype(f32)[:frames], head_lanes).astype(bf16)
        part = dot(cols_ref[c, :, :head_lanes], ga)
        values = part if values is None else values + part
    low = low_lanes(block)
    for pair in range(H // 2):
        q = qk_ref[:, pair * 256 : pair * 256 + 128].astype(f32)
        k = qk_ref[:, pair * 256 + 128 : pair * 256 + 256].astype(f32)
        v = values[:, pair * 128 : (pair + 1) * 128]
        qkv_out[:, pair * 384 : pair * 384 + 128] = jnp.where(low, q, k)
        qkv_out[:, pair * 384 + 128 : pair * 384 + 256] = jnp.where(low, v, q)
        qkv_out[:, pair * 384 + 256 : pair * 384 + 384] = jnp.where(low, k, v)


def params():
    return pltpu.CompilerParams(vmem_limit_bytes=56 << 20)


def shape(dims, kind):
    return jax.ShapeDtypeStruct(dims, kind)


VM = pl.BlockSpec(memory_space=pltpu.VMEM)
SM = pl.BlockSpec(memory_space=pltpu.SMEM)


def per_device(
    clip_tokens, attn_gain, qkv_weight, out_weight, head_gain, gloss_weight, gloss_targets, target_lengths
):
    seq_count = lax.axis_size("seq")
    clips = lax.axis_size("clip")
    me = lax.axis_index("seq")
    local, patches, width = clip_tokens.shape[1:]
    vocab = gloss_weight.shape[1]
    frames = local * seq_count
    here = up(-(-patches // seq_count), 16)
    rows = frames * here
    head_lanes = up(frames * H, 128)
    padded = up(frames, 8)
    block = width // seq_count
    gain_row = attn_gain.reshape(1, width)

    own = jnp.pad(clip_tokens[0], ((0, 0), (0, here * seq_count - patches), (0, 0)))
    x = lax.all_to_all(own, "seq", split_axis=1, concat_axis=0, tiled=True)
    q, k, v, probs, low, normed, inv, sums = pl.pallas_call(
        forward_kernel,
        out_shape=(
            shape((rows, width), bf16),
            shape((rows, width), bf16),
            shape((rows, width), bf16),
            shape((rows, head_lanes), f32),
            shape((rows, width), bf16),
            shape((rows, width), f32),
            shape((rows, 128), f32),
            shape((2, padded, width), f32),
        ),
        in_specs=[VM] * 3,
        out_specs=(VM,) * 8,
        compiler_params=params(),
        name="forward",
    )(x, gain_row, qkv_weight)
    all_sums = lax.all_gather(sums, "seq", axis=0)
    loss, frame_rows, gl, head_part, grad_mixed, mixed_low, ga, sum_att = pl.pallas_call(
        functools.partial(middle_kernel, patches, frames),
        out_shape=(
            shape((8, 128), f32),
            shape((padded, width), bf16),
            shape((padded, vocab), bf16),
            shape((8, width), f32),
            shape((padded, width), f32),
            shape((padded, width), bf16),
            shape((padded, width), bf16),
            shape((padded, width), f32),
        ),
        in_specs=[SM, SM] + [VM] * 4,
        out_specs=(VM,) * 8,
        compiler_params=params(),
        name="middle",
    )(gloss_targets, target_lengths, all_sums, out_weight, head_gain.reshape(1, width), gloss_weight)

    def cut(array):
        return lax.dynamic_slice_in_dim(array, me * block, block, 1)

    head8 = jnp.concatenate([head_part[:1], jnp.zeros((padded - 1, width), f32)], axis=0)
    packed = jnp.concatenate(
        [mixed_low, ga, gl, cut(frame_rows), cut(sum_att).astype(bf16), cut(head8).astype(bf16)], axis=1
    )
    gathered = lax.all_gather(packed, "clip", axis=0)
    gt, dw, cols = pl.pallas_call(
        functools.partial(backward_kernel, patches, frames, here),
        out_shape=(
            shape((frames, here, width), bf16),
            shape((width, 2 * width), bf16),
            shape((width, head_lanes + 128), bf16),
        ),
        in_specs=[VM] * 11,
        out_specs=(VM,) * 3,
        scratch_shapes=[pltpu.VMEM((rows, 2 * width), bf16)],
        compiler_params=params(),
        name="backward",
    )(q, k, v, probs, low, normed, inv, ga, grad_mixed, gain_row, qkv_weight)
    dw_own = lax.psum_scatter(dw, "seq", scatter_dimension=0, tiled=True)
    cols_own = lax.psum_scatter(cols, "seq", scatter_dimension=0, tiled=True)
    dw_sum = lax.psum(dw_own, "clip")
    cols_all = lax.all_gather(cols_own, "clip", axis=0)
    back = lax.all_to_all(gt, "seq", split_axis=0, concat_axis=1, tiled=True)
    grad_tokens = back[None, :, :patches]

    def part(start, size):
        return gathered[:, :, start : start + size]

    flat = clips * padded
    at = 2 * width + vocab
    qkv_share, out_share, gloss_share, head_share, gain_share = pl.pallas_call(
        functools.partial(final_kernel, frames),
        out_shape=(
            shape((block, 3 * width), f32),
            shape((block, width), f32),
            shape((block, vocab), f32),
            shape((1, block), f32),
            shape((block, 128), f32),
        ),
        in_specs=[VM] * 8,
        out_specs=(VM,) * 5,
        compiler_params=params(),
        name="final",
    )(
        dw_sum,
        cols_all,
        part(at + block, block).reshape(flat, block),
        part(0, width).reshape(flat, width),
        part(at, block).reshape(flat, block),
        part(2 * width, vocab).reshape(flat, vocab),
        part(width, width),
        part(at + 2 * block, block).reshape(flat, block),
    )
    return (
        loss[0, :1],
        grad_tokens,
        gain_share[:, 0],
        qkv_share,
        out_share,
        head_share[0],
        gloss_share,
    )


def solution(mesh):
    in_specs = (P("clip", "seq", None, None), P(), P(), P(), P(), P(), P("clip", None), P("clip"))
    out_specs = (
        P("clip"),
        P("clip", "seq", None, None),
        P("seq"),
        P("seq", None),
        P("seq", None),
        P("seq"),
        P("seq", None),
    )
    return jax.shard_map(
        per_device, mesh=mesh, in_specs=in_specs, out_specs=out_specs, check_vma=False
    )
```

profile of v0, /device:TPU:0, one launch (start us, length us, event | category | flops | bytes accessed | tf_op | source)
XLA Modules:
  0.0 277.2 jit_solution(7338208408666142902)
XLA Ops:
  7.2 1.6 copy.25
  8.8 1.0 pad_bitcast_fusion
  10.3 4.5 %reduce.2 = bf16[256,1024]{1,0:T(8,128)(2,1)} reduce(bf16[256,1,1024]{2,1,0:T(2,128)(2,1)S(1)} %pad_bitcast_fusion, bf16[]{:T(256)} %broadcast.15), dimensions={1}, to_apply=%pad_bitcast_fusion.reduce_sub_computation | reduce | bytes 1048578
  14.8 2.2 reshape.52
  17.0 4.2 %all-to-all-start = ((bf16[4,2,32768]{2,1,0:T(2,128)(2,1)}), bf16[4,2,32768]{2,1,0:T(2,128)(2,1)}, u32[]{:S(2)}, u32[]{:S(2)}) async-start(bf16[4,2,32768]{2,1,0:T(2,128)(2,1)} %reshape.52), calls=%async_computation | async-start | bytes 1048576 | tf_op jit(solution)/shard_map/all_to_all | solution.py:301
  21.9 2.7 copy.22.wg_ref
  24.6 6.1 %all-to-all-done = bf16[4,2,32768]{2,1,0:T(2,128)(2,1)} async-done(((bf16[4,2,32768]{2,1,0:T(2,128)(2,1)}), bf16[4,2,32768]{2,1,0:T(2,128)(2,1)}, u32[]{:S(2)}, u32[]{:S(2)}) %all-to-all-start) | async-done | bytes 524320 | tf_op jit(solution)/shard_map/all_to_all | solution.py:301
  30.7 2.2 reshape.53
  32.9 1.0 copy.24
  33.9 8.2 %forward.1 = (bf16[256,1024]{1,0:T(8,128)(2,1)}, bf16[256,1024]{1,0:T(8,128)(2,1)}, bf16[256,1024]{1,0:T(8,128)(2,1)}, f32[256,128]{1,0:T(8,128)}, bf16[256,1024...) custom-call(bf16[4,64,1024]{2,1,0:T(8,128)(2,1)} %bitcast.26, ...), custom_call_target="tpu_custom_call" | custom-call | tf_op jit(solution)/shard_map/forward/pallas_call | solution.py:302
  42.0 6.6 %all-gather = f32[8,8,1024]{2,1,0:T(8,128)} all-gather(f32[2,8,1024]{2,1,0:T(8,128)} %get-tuple-element.31), channel_id=2, replica_groups=mesh['clip'=8,'seq'=4] {'seq'}, dimensions={0}, use_global_device_ids=true | all-gather | bytes 327680 | tf_op jit(solution)/shard_map/all_gather | solution.py:319
  48.6 6.8 %middle.1 = (f32[8,128]{1,0:T(8,128)}, bf16[8,1024]{1,0:T(8,128)(2,1)}, bf16[8,1200]{1,0:T(8,128)(2,1)}, f32[8,1024]{1,0:T(8,128)}, f32[8,1024]{1,0:T(8,128)}, /...) custom-call(s32[1,2]{1,0:T(1,128)} %labels_ref.1, s32[1]{0:T(128)S(6)} %copy.27.length_ref, ...), custom_call_target="tpu_custom_call" | custom-call | tf_op jit(solution)/shard_map/middle/pallas_call | solution.py:320
  55.4 12.2 %backward.1 = (bf16[4,64,1024]{2,1,0:T(8,128)(2,1)}, bf16[1024,2048]{1,0:T(8,128)(2,1)}, bf16[1024,256]{1,0:T(8,128)(2,1)}) custom-call(bf16[256,1024]{1,0:T(8,128)(2,1)} %get-tuple-element.33.q_ref, bf16[256,1024]{1,0:T(8,128)(2,1)} %get-tuple-element.34.k_ref, bf16[256,1024]{1,0:T(8,128)(2,1)} %get-tuple-element.35.v_ref, ...), custom_call_target="tpu_custom_call" | custom-call | tf_op jit(solution)/shard_map/backward/pallas_call | solution.py:346
  68.4 23.0 %reduce-scatter.5.cloned.1.call-done = bf16[256,256]{1,0:T(8,128)(2,1)} async-done(((bf16[1024,256]{1,0:T(8,128)(2,1)}), bf16[256,256]{1,0:T(8,128)(2,1)}) %reduce-scatter.5.cloned.1.call-update) | async-done | bytes 131088 | tf_op jit(solution)/shard_map/reduce_scatter | solution.py:360
  93.1 31.3 %all-gather.2 = bf16[64,4016]{1,0:T(8,128)(2,1)S(1)} all-gather(bf16[8,4016]{1,0:T(8,128)(2,1)S(1)} %concatenate.7), channel_id=4, replica_groups=mesh['clip'=8,'seq'=4] {'clip'}, dimensions={0}, use_global_device_ids=true | all-gather | bytes 578304 | tf_op jit(solution)/shard_map/all_gather | solution.py:345
  124.4 14.3 %reduce-scatter.3.cloned.1.call-done = bf16[256,2048]{1,0:T(8,128)(2,1)} async-done(((bf16[1024,2048]{1,0:T(8,128)(2,1)}), bf16[256,2048]{1,0:T(8,128)(2,1)}) %reduce-scatter.3.cloned.1.call-update) | async-done | bytes 1048592 | tf_op jit(solution)/shard_map/reduce_scatter | solution.py:359
  139.4 1.2 slice.29
  140.6 3.5 %all-to-all-start.1 = ((bf16[4,64,1024]{2,1,0:T(8,128)(2,1)}), bf16[4,64,1024]{2,1,0:T(8,128)(2,1)S(1)}, u32[]{:S(2)}, u32[]{:S(2)}) async-start(bf16[4,64,1024]{2,1,0:T(8,128)(2,1)} %get-tuple-element.42), calls=%async_computation.1 | async-start | bytes 1048576 | tf_op jit(solution)/shard_map/all_to_all | solution.py:363
  145.5 7.4 %all-to-all-done.1 = bf16[4,64,1024]{2,1,0:T(8,128)(2,1)S(1)} async-done(((bf16[4,64,1024]{2,1,0:T(8,128)(2,1)}), bf16[4,64,1024]{2,1,0:T(8,128)(2,1)S(1)}, u32[]{:S(2)}, u32[]{:S(2)}) %all-to-all-start.1) | async-done | bytes 524320 | tf_op jit(solution)/shard_map/all_to_all | solution.py:363
  153.7 27.3 %all-gather.5.cloned.1.call-done = bf16[2048,256]{1,0:T(8,128)(2,1)} async-done(((bf16[256,256]{1,0:T(8,128)(2,1)}), bf16[2048,256]{1,0:T(8,128)(2,1)}) %all-gather.5.cloned.1.call-update) | async-done | bytes 1048592 | tf_op jit(solution)/shard_map/all_gather | solution.py:362
  181.0 80.3 %all-reduce.3.cloned.1.call-done.qk_ref = bf16[256,2048]{1,0:T(8,128)(2,1)} async-done(((bf16[256,2048]{1,0:T(8,128)(2,1)}), bf16[256,2048]{1,0:T(8,128)(2,1)}) %all-reduce.3.cloned.1.call-update) | async-done | bytes 1048592 | tf_op jit(solution)/shard_map/psum | solution.py:361
  261.3 5.0 %final.1 = (f32[256,3072]{1,0:T(8,128)}, f32[256,1024]{1,0:T(8,128)}, f32[256,1200]{1,0:T(8,128)}, f32[1,256]{1,0:T(1,128)}, f32[256,128]{1,0:T(8,128)}) custom-call(bf16[256,2048]{1,0:T(8,128)(2,1)} %all-reduce.3.cloned.1.call-done.qk_ref, bf16[8,256,256]{2,1,0:T(8,128)(2,1)} %bitcast.32, bf16[64,256]{1,0:T(8,128)(2,1)} %get-tuple-element.85.att_ref, ...), custom_call_target="tpu_custom_call" | custom-call | tf_op jit(solution)/shard_map/final/pallas_call | solution.py:371
  266.3 1.6 slice_reduce_fusion
  267.9 2.7 copy.23
  (26 shorter events, 5.9 us)
Async XLA Ops:
  8.8 13.1 %copy-start = (bf16[1024,1200]{0,1:T(8,128)(2,1)S(1)}, bf16[1024,1200]{0,1:T(8,128)(2,1)}, u32[]{:S(2)}) copy-start(bf16[1024,1200]{0,1:T(8,128)(2,1)} %param.13) | copy-start | bytes 7372804
  17.0 13.7 %all-to-all-start = ((bf16[4,2,32768]{2,1,0:T(2,128)(2,1)}), bf16[4,2,32768]{2,1,0:T(2,128)(2,1)}, u32[]{:S(2)}, u32[]{:S(2)}) async-start(bf16[4,2,32768]{2,1,0:T(2,128)(2,1)} %reshape.52), calls=%async_computation | async-start | bytes 1048576 | tf_op jit(solution)/shard_map/all_to_all | solution.py:301
  21.2 70.2 %reduce-scatter.5.cloned.1.call-start = ((), (), s32[]{:S(2)}) async-start(), calls=%async_computation.6 | async-start | bytes 655360 | tf_op jit(solution)/shard_map/reduce_scatter | solution.py:360
  67.6 24.6 %copy-start.4 = (pred[8]{0:T(512)(128)(4,1)S(1)}, pred[8]{0:T(512)(128)(4,1)}, u32[]{:S(2)}) copy-start(pred[8]{0:T(512)(128)(4,1)} %constant.14.clone.1) | copy-start | bytes 28
  67.6 25.4 %copy-start.1 = (bf16[8,1024]{1,0:T(8,128)(2,1)S(1)}, bf16[8,1024]{1,0:T(8,128)(2,1)}, u32[]{:S(2)}) copy-start(bf16[8,1024]{1,0:T(8,128)(2,1)} %get-tuple-element.40.ga_ref) | copy-start | bytes 49156
  67.6 25.4 %copy-start.2 = (bf16[8,1200]{1,0:T(8,128)(2,1)S(1)}, bf16[8,1200]{1,0:T(8,128)(2,1)}, u32[]{:S(2)}) copy-start(bf16[8,1200]{1,0:T(8,128)(2,1)} %get-tuple-element.46) | copy-start | bytes 57604
  67.6 25.4 %copy-start.3 = (bf16[8,1024]{1,0:T(8,128)(2,1)S(1)}, bf16[8,1024]{1,0:T(8,128)(2,1)}, u32[]{:S(2)}) copy-start(bf16[8,1024]{1,0:T(8,128)(2,1)} %get-tuple-element.45) | copy-start | bytes 49156
  67.6 71.1 %reduce-scatter.3.cloned.1.call-start = ((), (), s32[]{:S(2)}) async-start(), calls=%async_computation.4 | async-start | bytes 5242880 | tf_op jit(solution)/shard_map/reduce_scatter | solution.py:359
  68.4 112.6 %all-gather.5.cloned.1.call-start = ((), (), s32[]{:S(2)}) async-start(), calls=%async_computation.7 | async-start | bytes 1179648 | tf_op jit(solution)/shard_map/all_gather | solution.py:362
  91.5 169.8 %all-reduce.3.cloned.1.call-start = ((), (), s32[]{:S(2)}) async-start(), calls=%async_computation.5 | async-start | bytes 2097152 | tf_op jit(solution)/shard_map/psum | solution.py:361
  140.6 12.3 %all-to-all-start.1 = ((bf16[4,64,1024]{2,1,0:T(8,128)(2,1)}), bf16[4,64,1024]{2,1,0:T(8,128)(2,1)S(1)}, u32[]{:S(2)}, u32[]{:S(2)}) async-start(bf16[4,64,1024]{2,1,0:T(8,128)(2,1)} %get-tuple-element.42), calls=%async_computation.1 | async-start | bytes 1048576 | tf_op jit(solution)/shard_map/all_to_all | solution.py:363
Sparse Core Ops, SparseCore 0:
  67.7 23.6 reduce-scatter.4
  94.1 44.5 reduce-scatter.2
  140.8 40.1 all-gather.4
  184.3 76.9 all-reduce.2
where the time goes:
time: 278 us; the launch traced here: 277 us
  waiting for transfers between devices  159 us (57%)
  blocking collectives  37.9 us (14%)
  Pallas kernels  32.1 us (12%)
  local copies, waits for them, and re-layouts  20.3 us (7%)
  between operations  14.5 us (5%)
  starting transfers between devices  7.83 us (3%)
  other arithmetic  5.27 us (2%)
    psum x1, waiting for transfers between devices, per_device(): dw_sum = lax.psum(dw_own, 'clip')  80.3 us
    all_gather x1, blocking collectives, per_device(): gathered = lax.all_gather(packed, 'clip', axis=0)  31.3 us
    all_gather x1, waiting for transfers between devices, per_device(): cols_all = lax.all_gather(cols_own, 'clip', axis=0)  27.3 us
    reduce_scatter x1, waiting for transfers between devices, per_device(): cols_own = lax.psum_scatter(cols, 'seq', scatter_dimension=0, tiled=True)  23 us
    reduce_scatter x1, waiting for transfers between devices, per_device(): dw_own = lax.psum_scatter(dw, 'seq', scatter_dimension=0, tiled=True)  14.3 us
    unnamed x18, local copies, waits for them, and re-layouts  13.9 us
    pallas_call x1, Pallas kernels, per_device(): pl.pallas_call(functools.partial(backward_kernel, patches, frames, here),...  12.2 us
    pallas_call x1, Pallas kernels, per_device(): pl.pallas_call(forward_kernel, out_shape=(shape((rows, width), bf16), sha...  8.16 us
  transfers between devices with their start and end apart: 6, of which 6 were waited for; matrix products, arithmetic and copies ran while one was open for 3% of the time, Pallas kernels for 0%

commit v1 on v0

--- a/solution.py
+++ b/solution.py
@@ -230,10 +230,19 @@
         dw_ref[:, start : start + chunk] = dot(
             tokens_low, qk_ref[:, start : start + chunk], ((0,), (0,))
         ).astype(bf16)
-    cols_ref[:, :head_lanes] = dot(tokens_low, probs_low, ((0,), (0,))).astype(bf16)
+    coefs = dot(tokens_low, probs_low, ((0,), (0,)))
     normed = norm_ref[...]
     gain_part = (grad_normed * normed).astype(bf16)
-    cols_ref[:, head_lanes:] = dot(gain_part, jnp.ones((rows, 128), bf16), ((0,), (0,))).astype(bf16)
+    gain_cols = dot(gain_part, jnp.ones((rows, 128), bf16), ((0,), (0,)))
+    if frames * H < head_lanes:
+        lane = lax.broadcasted_iota(jnp.int32, (width, 128), 1)
+        tail = head_lanes - 128
+        if tail:
+            cols_ref[:, :tail] = coefs[:, :tail].astype(bf16)
+        cols_ref[:, tail:] = jnp.where(lane < frames * H - tail, coefs[:, tail:], gain_cols).astype(bf16)
+    else:
+        cols_ref[:, :head_lanes] = coefs.astype(bf16)
+        cols_ref[:, head_lanes:] = gain_cols.astype(bf16)
     scaled = grad_normed * gain_ref[...]
     back = inv_ref[:, :1] * (
         scaled
@@ -249,11 +258,11 @@
     qkv_out, out_out, gloss_out, head_out, gain_out,
 ):
     clips, block, lanes = cols_ref.shape
-    head_lanes = lanes - 128
+    head_lanes = up(frames * H, 128)
     out_out[...] = dot(att_ref[...], mix_ref[...], ((0,), (0,)))
     gloss_out[...] = dot(frame_ref[...], gl_ref[...], ((0,), (0,)))
     head_out[...] = jnp.sum(head_ref[...].astype(f32), axis=0, keepdims=True)
-    gain_out[...] = jnp.sum(cols_ref[:, :, head_lanes:].astype(f32), axis=0)
+    gain_out[...] = jnp.sum(cols_ref[:, :, lanes - 128 :].astype(f32), axis=0)
     values = None
     for c in range(clips):
         ga = by_head(ga_ref[c].astype(f32)[:frames], head_lanes).astype(bf16)
@@ -269,6 +278,220 @@
         qkv_out[:, pair * 384 + 256 : pair * 384 + 384] = jnp.where(low, k, v)
 
 
+def exchange_scratch(seq_count, clips, block, width, lanes, chunk_count):
+    pairs, half = seq_count // 2, clips // 2
+    wide = 2 * width + lanes
+    piece = 2 * width // clips
+    sems = pltpu.SemaphoreType.DMA
+    return [
+        pltpu.VMEM((pairs, block, wide), bf16),
+        pltpu.VMEM((pairs, block, wide), bf16),
+        pltpu.VMEM((pairs - 1, block, wide), bf16),
+        pltpu.VMEM((block, wide), bf16),
+        pltpu.VMEM((block, width), bf16),
+        pltpu.VMEM((block, width), bf16),
+        pltpu.VMEM((half - 1, block, piece), bf16),
+        sems((2, seq_count - 1)),
+        sems((2, half)),
+        sems((2, chunk_count, 2 * pairs)),
+        sems((2, chunk_count, pairs - 1)),
+        sems((2, chunk_count)),
+        sems((2, chunk_count, half - 1)),
+        sems((2, chunk_count, half - 1)),
+        sems((2, chunk_count, half - 1)),
+        sems((2, chunk_count, 2)),
+    ]
+
+
+def exchange_kernel(
+    chunk_count, dw_ref, cols_ref, rows_ref, gt_ref, sum_ref, all_cols_ref, all_rows_ref, back_ref,
+    core_in, core_sum, pair_in, seq_sum, x_in, x_sum, z_in,
+    token_sem, row_sem, core_sem, pair_sem, x_sem, z_sem, zq_sem, zc_sem, xg_sem,
+):
+    seq_count, local = back_ref.shape[:2]
+    half = all_cols_ref.shape[1]
+    pairs = seq_count // 2
+    block, full = sum_ref.shape
+    width = full // 2
+    piece = width // half
+    size = block // chunk_count
+    me = lax.axis_index("seq")
+    clip = lax.axis_index("clip")
+    core, hi = lax.rem(me, 2), me // 2
+    x, z = lax.rem(clip, 2), clip // 2
+
+    def at(clip_id, seq_id):
+        return (clip_id, seq_id)
+
+    sibling = at(clip, hi * 2 + (1 - core))
+    x_peer = at(z * 2 + (1 - x), me)
+
+    def z_peer(step):
+        return at(lax.rem(z + step, half) * 2 + x, me)
+
+    barrier = pltpu.get_barrier_semaphore()
+    peers = [at(clip, lax.rem(me + step, seq_count)) for step in range(1, seq_count)]
+    peers += [x_peer] + [z_peer(step) for step in range(1, half)]
+    for peer in peers:
+        pl.semaphore_signal(barrier, inc=1, device_id=peer, device_id_type=pl.DeviceIdType.MESH)
+    pl.semaphore_wait(barrier, len(peers))
+
+    started = []
+
+    def send(src, dst, sems, index, peer):
+        copy = pltpu.make_async_remote_copy(
+            src_ref=src,
+            dst_ref=dst,
+            send_sem=sems.at[(0,) + index],
+            recv_sem=sems.at[(1,) + index],
+            device_id=peer,
+            device_id_type=pl.DeviceIdType.MESH,
+        )
+        copy.start()
+        started.append(copy)
+        return copy
+
+    waits = {}
+
+    def rows(c):
+        return pl.ds(c * size, size)
+
+    def block_rows(index, c):
+        return pl.ds(pl.multiple_of(index * block + c * size, 16), size)
+
+    def half_cols(index):
+        return pl.ds(pl.multiple_of(index * width, 128), width)
+
+    def first(c):
+        waits[1, c] = []
+        for p in range(pairs):
+            src = block_rows(p * 2 + (1 - core), c)
+            waits[1, c] += [
+                send(dw_ref.at[src], core_in.at[p, rows(c), pl.ds(0, full)], core_sem, (c, 2 * p), sibling),
+                send(
+                    cols_ref.at[src],
+                    core_in.at[p, rows(c), pl.ds(full, cols_ref.shape[1])],
+                    core_sem,
+                    (c, 2 * p + 1),
+                    sibling,
+                ),
+            ]
+
+    def second(c):
+        for copy in waits[1, c]:
+            copy.wait_recv()
+        for p in range(pairs):
+            own = block_rows(p * 2 + core, c)
+            core_sum[p, rows(c), :full] = dw_ref[own, :] + core_in[p, rows(c), :full]
+            core_sum[p, rows(c), full:] = cols_ref[own, :] + core_in[p, rows(c), full:]
+        waits[2, c] = [
+            send(
+                core_sum.at[lax.rem(hi + step, pairs), rows(c)],
+                pair_in.at[step - 1, rows(c)],
+                pair_sem,
+                (c, step - 1),
+                at(clip, lax.rem(hi + step, pairs) * 2 + core),
+            )
+            for step in range(1, pairs)
+        ]
+
+    def third(c):
+        for copy in waits[2, c]:
+            copy.wait_recv()
+        total = core_sum[hi, rows(c)].astype(f32)
+        for step in range(pairs - 1):
+            total += pair_in[step, rows(c)].astype(f32)
+        total = total.astype(bf16)
+        seq_sum[rows(c)] = total
+        all_cols_ref[x, z, rows(c)] = total[:, full:]
+        waits[3, c] = [
+            send(seq_sum.at[rows(c), half_cols(1 - x)], x_in.at[rows(c)], x_sem, (c,), x_peer)
+        ]
+        waits[5, c] = [
+            send(
+                all_cols_ref.at[x, z, rows(c)],
+                all_cols_ref.at[x, z, rows(c)],
+                zc_sem,
+                (c, step - 1),
+                z_peer(step),
+            )
+            for step in range(1, half)
+        ]
+
+    def fourth(c):
+        for copy in waits[3, c]:
+            copy.wait_recv()
+        x_sum[rows(c)] = seq_sum[rows(c), half_cols(x)] + x_in[rows(c)]
+        waits[4, c] = [
+            send(
+                x_sum.at[rows(c), pl.ds(pl.multiple_of(lax.rem(z + step, half) * piece, 128), piece)],
+                z_in.at[step - 1, rows(c)],
+                z_sem,
+                (c, step - 1),
+                z_peer(step),
+            )
+            for step in range(1, half)
+        ]
+
+    def fifth(c):
+        for copy in waits[4, c]:
+            copy.wait_recv()
+        total = x_sum[rows(c), pl.ds(pl.multiple_of(z * piece, 128), piece)].astype(f32)
+        for step in range(half - 1):
+            total += z_in[step, rows(c)].astype(f32)
+        own = pl.ds(pl.multiple_of(x * width + z * piece, 128), piece)
+        sum_ref[rows(c), own] = total.astype(bf16)
+        waits[5, c] += [
+            send(
+                sum_ref.at[rows(c), own], sum_ref.at[rows(c), own], zq_sem, (c, step - 1), z_peer(step)
+            )
+            for step in range(1, half)
+        ]
+
+    def sixth(c):
+        for copy in waits[5, c]:
+            copy.wait_recv()
+        mine = (rows(c), half_cols(x))
+        waits[6, c] = [
+            send(sum_ref.at[mine], sum_ref.at[mine], xg_sem, (c, 0), x_peer),
+            send(
+                all_cols_ref.at[x, :, rows(c)], all_cols_ref.at[x, :, rows(c)], xg_sem, (c, 1), x_peer
+            ),
+        ]
+
+    def seventh(c):
+        for copy in waits[6, c]:
+            copy.wait_recv()
+
+    stages = [first, second, third, fourth, fifth, sixth, seventh]
+    for c in range(chunk_count):
+        first(c)
+    all_rows_ref[x, z] = rows_ref[...]
+    row_waits = [
+        send(rows_ref, all_rows_ref.at[x, z], row_sem, (step - 1,), z_peer(step))
+        for step in range(1, half)
+    ]
+    token_waits = []
+    for step in range(1, seq_count):
+        to = lax.rem(me + step, seq_count)
+        token_waits.append(
+            send(gt_ref.at[pl.ds(to * local, local)], back_ref.at[me], token_sem, (step - 1,), at(clip, to))
+        )
+    back_ref[me] = gt_ref[pl.ds(me * local, local)]
+    for wave in range(1, chunk_count + len(stages) - 1):
+        for c in range(chunk_count):
+            if 1 <= wave - c < len(stages):
+                stages[wave - c](c)
+        if wave == 2:
+            for copy in row_waits:
+                copy.wait_recv()
+            row_waits = [send(all_rows_ref.at[x], all_rows_ref.at[x], row_sem, (half - 1,), x_peer)]
+    for copy in row_waits + token_waits:
+        copy.wait_recv()
+    for copy in started:
+        copy.wait_send()
+
+
 def params():
     return pltpu.CompilerParams(vmem_limit_bytes=56 << 20)
 
@@ -293,6 +516,7 @@
     here = up(-(-patches // seq_count), 16)
     rows = frames * here
     head_lanes = up(frames * H, 128)
+    lanes = up(frames * H + 1, 128)
     padded = up(frames, 8)
     block = width // seq_count
     gain_row = attn_gain.reshape(1, width)
@@ -342,13 +566,12 @@
     packed = jnp.concatenate(
         [mixed_low, ga, gl, cut(frame_rows), cut(sum_att).astype(bf16), cut(head8).astype(bf16)], axis=1
     )
-    gathered = lax.all_gather(packed, "clip", axis=0)
     gt, dw, cols = pl.pallas_call(
         functools.partial(backward_kernel, patches, frames, here),
         out_shape=(
             shape((frames, here, width), bf16),
             shape((width, 2 * width), bf16),
-            shape((width, head_lanes + 128), bf16),
+            shape((width, lanes), bf16),
         ),
         in_specs=[VM] * 11,
         out_specs=(VM,) * 3,
@@ -356,11 +579,27 @@
         compiler_params=params(),
         name="backward",
     )(q, k, v, probs, low, normed, inv, ga, grad_mixed, gain_row, qkv_weight)
-    dw_own = lax.psum_scatter(dw, "seq", scatter_dimension=0, tiled=True)
-    cols_own = lax.psum_scatter(cols, "seq", scatter_dimension=0, tiled=True)
-    dw_sum = lax.psum(dw_own, "clip")
-    cols_all = lax.all_gather(cols_own, "clip", axis=0)
-    back = lax.all_to_all(gt, "seq", split_axis=0, concat_axis=1, tiled=True)
+    half = clips // 2
+    chunk_count = 4
+    dw_sum, cols_all, gathered, back = pl.pallas_call(
+        functools.partial(exchange_kernel, chunk_count),
+        out_shape=(
+            shape((block, 2 * width), bf16),
+            shape((2, half, block, lanes), bf16),
+            shape((2, half) + packed.shape, bf16),
+            shape((seq_count, local, here, width), bf16),
+        ),
+        in_specs=[VM] * 4,
+        out_specs=(VM,) * 4,
+        scratch_shapes=exchange_scratch(seq_count, clips, block, width, lanes, chunk_count),
+        compiler_params=pltpu.CompilerParams(
+            vmem_limit_bytes=56 << 20, collective_id=0, has_side_effects=True
+        ),
+        name="exchange",
+    )(dw, cols, packed, gt)
+    cols_all = cols_all.reshape(clips, block, lanes)
+    gathered = gathered.reshape((clips,) + packed.shape)
+    back = back.transpose(1, 0, 2, 3).reshape(local, seq_count * here, width)
     grad_tokens = back[None, :, :patches]
 
     def part(start, size):
@@ -394,7 +633,7 @@
     return (
         loss[0, :1],
         grad_tokens,
-        gain_share[:, 0],
+        gain_share[:, 127],
         qkv_share,
         out_share,
         head_share[0],

time: 278 us -> 148 us (0.53)
  waiting for transfers between devices: 159 us -> 6.12 us
  Pallas kernels: 32.1 us -> 97.7 us
  blocking collectives: 37.9 us -> 6.74 us
  between operations: 14.5 us -> 1.34 us
  local copies, waits for them, and re-layouts: 20.3 us -> 25.5 us
  starting transfers between devices: 7.83 us -> 4.24 us
    psum x1 -> x0, waiting for transfers between devices: 80.3 us -> none  [per_device(): dw_sum = lax.psum(dw_own, 'clip')]
    pallas_call x0 -> x1, Pallas kernels: none -> 65.8 us  [per_device(): pl.pallas_call(functools.partial(exchange_kernel, chunk_count), out_shape...]
    reduce_scatter x2 -> x0, waiting for transfers between devices: 37.3 us -> none  [the longest x1 23 us: per_device(): cols_own = lax.psum_scatter(cols, 'seq', scatter_dimension=0, tiled=True)]
    all_gather x1 -> x0, blocking collectives: 31.3 us -> none  [per_device(): gathered = lax.all_gather(packed, 'clip', axis=0)]
    all_gather x1 -> x0, waiting for transfers between devices: 27.3 us -> none  [per_device(): cols_all = lax.all_gather(cols_own, 'clip', axis=0)]
    all_to_all x1 -> x0, waiting for transfers between devices: 7.42 us -> none  [per_device(): back = lax.all_to_all(gt, 'seq', split_axis=0, concat_axis=1, tiled=True)]
    all_to_all x1 -> x0, starting transfers between devices: 3.47 us -> none  [per_device(): back = lax.all_to_all(gt, 'seq', split_axis=0, concat_axis=1, tiled=True)]
    unnamed x18 -> x12, local copies, waits for them, and re-layouts: 13.9 us -> 13.9 us
  transfers between devices with their start and end apart: 6 -> 1, of which waited for: 6 -> 1; matrix products, arithmetic and copies ran while one was open for 3% -> 2% of each run, Pallas kernels for 0% -> 0%
where the time goes in v1:
time: 148 us; the launch traced here: 147 us
  Pallas kernels  97.7 us (66%)
  local copies, waits for them, and re-layouts  25.5 us (17%)
  blocking collectives  6.74 us (5%)
  waiting for transfers between devices  6.12 us (4%)
  other arithmetic  5.27 us (4%)
  starting transfers between devices  4.24 us (3%)
    pallas_call x1, Pallas kernels, per_device(): pl.pallas_call(functools.partial(exchange_kernel, chunk_count), out_shape...  65.8 us
    unnamed x12, local copies, waits for them, and re-layouts  13.9 us
    pallas_call x1, Pallas kernels, per_device(): pl.pallas_call(functools.partial(backward_kernel, patches, frames, here),...  12.1 us
    pallas_call x1, Pallas kernels, per_device(): pl.pallas_call(forward_kernel, out_shape=(shape((rows, width), bf16), sha...  8.17 us
    pallas_call x1, Pallas kernels, per_device(): pl.pallas_call(functools.partial(middle_kernel, patches, frames), out_sha...  6.77 us
    all_gather x1, blocking collectives, per_device(): all_sums = lax.all_gather(sums, 'seq', axis=0)  6.74 us
    all_to_all x1, waiting for transfers between devices, per_device(): x = lax.all_to_all(own, 'seq', split_axis=1, concat_axis=0, tiled=True)  6.12 us
    pallas_call x1, Pallas kernels, per_device(): pl.pallas_call(functools.partial(final_kernel, frames), out_shape=(shape(...  4.86 us
  transfers between devices with their start and end apart: 1, of which 1 were waited for; matrix products, arithmetic and copies ran while one was open for 2% of the time, Pallas kernels for 0%

profile of v1, /device:TPU:0, one launch (start us, length us, event | category | flops | bytes accessed | tf_op | source)
XLA Modules:
  0.0 146.9 jit_solution(7340823096617489225)
XLA Ops:
  0.6 1.6 %copy.25 = bf16[1,196,1024]{2,0,1:T(2,128)(2,1)S(1)} copy(bf16[1,196,1024]{2,1,0:T(8,128)(2,1)} %bitcast.32) | data formatting | bytes 802816
  2.3 1.0 pad_bitcast_fusion
  3.7 4.5 %reduce.2 = bf16[256,1024]{1,0:T(8,128)(2,1)} reduce(bf16[256,1,1024]{2,1,0:T(2,128)(2,1)S(1)} %pad_bitcast_fusion, bf16[]{:T(256)} %broadcast.15), dimensions={1}, to_apply=%pad_bitcast_fusion.reduce_sub_computation | reduce | bytes 1048578
  8.2 2.2 %reshape.55 = bf16[4,2,32768]{2,1,0:T(2,128)(2,1)} reshape(bf16[256,1024]{1,0:T(8,128)(2,1)} %reduce.2) | data formatting | bytes 1048576
  10.5 4.2 %all-to-all-start = ((bf16[4,2,32768]{2,1,0:T(2,128)(2,1)}), bf16[4,2,32768]{2,1,0:T(2,128)(2,1)}, u32[]{:S(2)}, u32[]{:S(2)}) async-start(bf16[4,2,32768]{2,1,0:T(2,128)(2,1)} %reshape.55), calls=%async_computation | async-start | bytes 1048576 | tf_op jit(solution)/shard_map/all_to_all | solution.py:525
  15.3 2.7 %copy.22.wg_ref = bf16[1024,1200]{1,0:T(8,128)(2,1)} copy(bf16[1024,1200]{0,1:T(8,128)(2,1)S(1)} %copy-done) | data formatting | bytes 4915200 | tf_op args[5]
  18.0 6.1 %all-to-all-done = bf16[4,2,32768]{2,1,0:T(2,128)(2,1)} async-done(((bf16[4,2,32768]{2,1,0:T(2,128)(2,1)}), bf16[4,2,32768]{2,1,0:T(2,128)(2,1)}, u32[]{:S(2)}, u32[]{:S(2)}) %all-to-all-start) | async-done | bytes 524320 | tf_op jit(solution)/shard_map/all_to_all | solution.py:525
  24.1 2.2 %reshape.56 = bf16[256,1,1024]{2,1,0:T(2,128)(2,1)S(1)} reshape(bf16[4,2,32768]{2,1,0:T(2,128)(2,1)} %all-to-all-done) | data formatting | bytes 1048576
  26.4 1.0 copy.24
  27.3 8.2 %forward.1 = (bf16[256,1024]{1,0:T(8,128)(2,1)}, bf16[256,1024]{1,0:T(8,128)(2,1)}, bf16[256,1024]{1,0:T(8,128)(2,1)}, f32[256,128]{1,0:T(8,128)}, bf16[256,1024...) custom-call(bf16[4,64,1024]{2,1,0:T(8,128)(2,1)} %bitcast.26, ...), custom_call_target="tpu_custom_call" | custom-call | tf_op jit(solution)/shard_map/forward/pallas_call | solution.py:526
  35.5 6.7 %all-gather = f32[8,8,1024]{2,1,0:T(8,128)} all-gather(f32[2,8,1024]{2,1,0:T(8,128)} %get-tuple-element.35), channel_id=2, replica_groups=mesh['clip'=8,'seq'=4] {'seq'}, dimensions={0}, use_global_device_ids=true | all-gather | bytes 327680 | tf_op jit(solution)/shard_map/all_gather | solution.py:543
  42.2 6.8 %middle.1 = (f32[8,128]{1,0:T(8,128)}, bf16[8,1024]{1,0:T(8,128)(2,1)}, bf16[8,1200]{1,0:T(8,128)(2,1)}, f32[8,1024]{1,0:T(8,128)}, f32[8,1024]{1,0:T(8,128)}, /...) custom-call(s32[1,2]{1,0:T(1,128)} %labels_ref.1, s32[1]{0:T(128)S(6)} %copy.26.length_ref, ...), custom_call_target="tpu_custom_call" | custom-call | tf_op jit(solution)/shard_map/middle/pallas_call | solution.py:544
  49.7 0.8 fusion
  50.5 1.5 %concatenate.7.rows_ref = bf16[8,4016]{1,0:T(8,128)(2,1)} concatenate(bf16[8,1024]{1,0:T(8,128)(2,1)} %get-tuple-element.48, bf16[8,1024]{1,0:T(8,128)(2,1)} %get-tuple-element.44.ga_ref, bf16[8,1200]{1,0:T(8,128)(2,1)} %get-tuple-element.49, bf16[8,256]{1,0:T(8,128)(2,1)S(1)} %constant_dynamic-slice_fusion, bf16[8,256]{1,0:T(8,128)(2,1)S(1)} %get-tuple-element.97, ...), dimensions={1} | concatenate | bytes 128512 | tf_op jit(solution)/shard_map/concatenate | solution.py:566
  52.0 12.1 %backward.1 = (bf16[4,64,1024]{2,1,0:T(8,128)(2,1)}, bf16[1024,2048]{1,0:T(8,128)(2,1)}, bf16[1024,128]{1,0:T(8,128)(2,1)}) custom-call(bf16[256,1024]{1,0:T(8,128)(2,1)} %get-tuple-element.37.q_ref, bf16[256,1024]{1,0:T(8,128)(2,1)} %get-tuple-element.38.k_ref, bf16[256,1024]{1,0:T(8,128)(2,1)} %get-tuple-element.39.v_ref, ...), custom_call_target="tpu_custom_call" | custom-call | tf_op jit(solution)/shard_map/backward/pallas_call | solution.py:569
  64.0 65.8 %exchange.1 = (bf16[256,2048]{1,0:T(8,128)(2,1)}, bf16[2,4,256,128]{3,2,1,0:T(8,128)(2,1)}, bf16[2,4,8,4016]{3,2,1,0:T(8,128)(2,1)}, bf16[4,1,64,1024]{3,2,1,0:T(8,128)(2,1)}) custom-call(bf16[1024,2048]{1,0:T(8,128)(2,1)} %get-tuple-element.46.dw_ref, bf16[1024,128]{1,0:T(8,128)(2,1)} %get-tuple-element.47.cols_ref, bf16[8,4016]{1,0:T(8,128)(2,1)} %concatenate.7.rows_ref, ...), custom_call_target="tpu_custom_call" | custom-call | tf_op jit(solution)/shard_map/exchange/pallas_call | solution.py:584
  129.8 1.6 %slice_bitcast_fusion.3 = (bf16[64,256]{1,0:T(8,128)(2,1)}, bf16[64,256]{1,0:T(8,128)(2,1)}, bf16[64,256]{1,0:T(8,128)(2,1)}) fusion(bf16[8,8,4016]{2,1,0:T(8,128)(2,1)} %bitcast.28), kind=kLoop, calls=%fused_computation.4 | loop fusion | bytes 196608 | tf_op jit(solution)/shard_map/reshape | solution.py:631
  131.4 1.6 %slice_bitcast_fusion.1.gl_ref = bf16[64,1200]{1,0:T(8,128)(2,1)} fusion(bf16[8,8,4016]{2,1,0:T(8,128)(2,1)} %bitcast.29), kind=kLoop, calls=%fused_computation.1 | loop fusion | bytes 307200 | tf_op jit(solution)/shard_map/reshape | solution.py:629
  133.0 1.7 %fusion.1 = (bf16[8,8,1024]{2,1,0:T(8,128)(2,1)}, bf16[64,1024]{1,0:T(8,128)(2,1)}) fusion(bf16[8,8,4016]{2,1,0:T(8,128)(2,1)} %bitcast.30), kind=kLoop, calls=%fused_computation.11 | loop fusion | bytes 524288 | tf_op jit(solution)/shard_map/slice | solution.py:606
  134.7 1.2 slice.29
  135.9 1.8 %slice_bitcast_fusion = bf16[1,1,196,1024]{3,2,1,0:T(8,128)(2,1)} fusion(bf16[1,256,1024]{2,1,0:T(8,128)(2,1)} %bitcast.33), kind=kLoop, calls=%fused_computation | loop fusion | bytes 802816 | tf_op jit(solution)/shard_map/broadcast_in_dim | solution.py:603
  137.7 4.9 %final.1 = (f32[256,3072]{1,0:T(8,128)}, f32[256,1024]{1,0:T(8,128)}, f32[256,1200]{1,0:T(8,128)}, f32[1,256]{1,0:T(1,128)}, f32[256,128]{1,0:T(8,128)}) custom-call(bf16[256,2048]{1,0:T(8,128)(2,1)} %get-tuple-element.55.qk_ref, bf16[8,256,128]{2,1,0:T(8,128)(2,1)} %bitcast.31, bf16[64,256]{1,0:T(8,128)(2,1)} %get-tuple-element.93.att_ref, ...), custom_call_target="tpu_custom_call" | custom-call | tf_op jit(solution)/shard_map/final/pallas_call | solution.py:610
  142.5 1.6 %slice_reduce_fusion = f32[256]{0:T(256)} fusion(f32[256,128]{1,0:T(8,128)} %get-tuple-element.58), kind=kLoop, calls=%fused_computation.3 | loop fusion | bytes 2048 | tf_op jit(solution)/shard_map/slice | solution.py:636
  144.2 2.7 %copy.23 = f32[256,1200]{0,1:T(8,128)} copy(f32[256,1200]{1,0:T(8,128)} %get-tuple-element.90) | data formatting | bytes 2457600
  (6 shorter events, 1.2 us)
Async XLA Ops:
  2.3 13.1 %copy-start = (bf16[1024,1200]{0,1:T(8,128)(2,1)S(1)}, bf16[1024,1200]{0,1:T(8,128)(2,1)}, u32[]{:S(2)}) copy-start(bf16[1024,1200]{0,1:T(8,128)(2,1)} %param.13) | copy-start | bytes 7372804
  10.5 13.7 %all-to-all-start = ((bf16[4,2,32768]{2,1,0:T(2,128)(2,1)}), bf16[4,2,32768]{2,1,0:T(2,128)(2,1)}, u32[]{:S(2)}, u32[]{:S(2)}) async-start(bf16[4,2,32768]{2,1,0:T(2,128)(2,1)} %reshape.55), calls=%async_computation | async-start | bytes 1048576 | tf_op jit(solution)/shard_map/all_to_all | solution.py:525
  35.5 14.2 %copy-start.1 = (pred[8]{0:T(512)(128)(4,1)S(1)}, pred[8]{0:T(512)(128)(4,1)}, u32[]{:S(2)}) copy-start(pred[8]{0:T(512)(128)(4,1)} %constant.14.clone.1) | copy-start | bytes 28

commit v2 on v1

--- a/solution.py
+++ b/solution.py
@@ -48,8 +48,50 @@
     return lax.broadcasted_iota(jnp.int32, (rows, 128), 1) < HD
 
 
-def forward_kernel(x_ref, gain_ref, w_ref, q_ref, k_ref, v_ref, p_ref, low_ref, norm_ref, inv_ref, sum_ref):
+def forward_kernel(
+    own_ref, gain_ref, w_hbm, q_ref, k_ref, v_ref, p_ref, low_ref, norm_ref, inv_ref, all_sums_ref,
+    x_ref, w_ref, w_sem, token_sem, sums_sem,
+):
     frames, here, width = x_ref.shape
+    local = own_ref.shape[0]
+    seq_count = frames // local
+    me = lax.axis_index("seq")
+    clip = lax.axis_index("clip")
+    w_copy = pltpu.make_async_copy(w_hbm, w_ref, w_sem)
+    w_copy.start()
+    barrier = pltpu.get_barrier_semaphore()
+    for step in range(1, seq_count):
+        pl.semaphore_signal(
+            barrier,
+            inc=1,
+            device_id=(clip, lax.rem(me + step, seq_count)),
+            device_id_type=pl.DeviceIdType.MESH,
+        )
+    pl.semaphore_wait(barrier, seq_count - 1)
+
+    def send(src, dst, sems, step):
+        copy = pltpu.make_async_remote_copy(
+            src_ref=src,
+            dst_ref=dst,
+            send_sem=sems.at[0, step - 1],
+            recv_sem=sems.at[1, step - 1],
+            device_id=(clip, lax.rem(me + step, seq_count)),
+            device_id_type=pl.DeviceIdType.MESH,
+        )
+        copy.start()
+        return copy
+
+    def patch_rows(device):
+        return pl.ds(pl.multiple_of(device * here, 16), here)
+
+    mine = pl.ds(me * local, local)
+    tokens = [
+        send(own_ref.at[:, patch_rows(lax.rem(me + step, seq_count))], x_ref.at[mine], token_sem, step)
+        for step in range(1, seq_count)
+    ]
+    x_ref[mine] = own_ref[:, patch_rows(me)]
+    for copy in tokens:
+        copy.wait_recv()
     rows = frames * here
     head_lanes = p_ref.shape[1]
     x = x_ref[...].reshape(rows, width).astype(f32)
@@ -60,6 +102,7 @@
     inv_ref[...] = jnp.broadcast_to(inv, (rows, 128))
     low_ref[...] = (normed * gain_ref[...]).astype(bf16)
     low = low_lanes(rows)
+    w_copy.wait()
     for pair in range(H // 2):
         y = dot(low_ref[...], w_ref[:, pair * 384 : (pair + 1) * 384])
         a, b, c = y[:, :128], y[:, 128:256], y[:, 256:]
@@ -81,12 +124,20 @@
     row = lax.broadcasted_iota(jnp.int32, (H, width), 0)
     col = lax.broadcasted_iota(jnp.int32, (H, width), 1)
     own = row == lax.shift_right_logical(col, 6)
-    sum_ref[...] = jnp.zeros_like(sum_ref)
-    for t in range(frames):
-        sum_ref[0, t : t + 1, :] = jnp.sum(x[t * here : (t + 1) * here], axis=0, keepdims=True)
-        sum_ref[1, t : t + 1, :] = jnp.sum(
-            jnp.where(own, mixed[t * H : (t + 1) * H], 0.0), axis=0, keepdims=True
-        )
+    padded = all_sums_ref.shape[2]
+    blank = [jnp.zeros((padded - frames, width), f32)] if padded > frames else []
+    tok = [jnp.sum(x[t * here : (t + 1) * here], axis=0, keepdims=True) for t in range(frames)]
+    att = [
+        jnp.sum(jnp.where(own, mixed[t * H : (t + 1) * H], 0.0), axis=0, keepdims=True)
+        for t in range(frames)
+    ]
+    all_sums_ref[me, 0] = jnp.concatenate(tok + blank, axis=0)
+    all_sums_ref[me, 1] = jnp.concatenate(att + blank, axis=0)
+    sums = [send(all_sums_ref.at[me], all_sums_ref.at[me], sums_sem, step) for step in range(1, seq_count)]
+    for copy in sums:
+        copy.wait_recv()
+    for copy in tokens + sums:
+        copy.wait_send()
 
 
 def add_log(left, right):
@@ -254,18 +305,30 @@
 
 
 def final_kernel(
-    frames, qk_ref, cols_ref, att_ref, mix_ref, frame_ref, gl_ref, ga_ref, head_ref,
+    frames, qk_ref, cols_ref, rows_ref,
     qkv_out, out_out, gloss_out, head_out, gain_out,
 ):
     clips, block, lanes = cols_ref.shape
     head_lanes = up(frames * H, 128)
-    out_out[...] = dot(att_ref[...], mix_ref[...], ((0,), (0,)))
-    gloss_out[...] = dot(frame_ref[...], gl_ref[...], ((0,), (0,)))
-    head_out[...] = jnp.sum(head_ref[...].astype(f32), axis=0, keepdims=True)
-    gain_out[...] = jnp.sum(cols_ref[:, :, lanes - 128 :].astype(f32), axis=0)
+    padded = rows_ref.shape[1]
+    width, vocab = out_out.shape[1], gloss_out.shape[1]
+    step = up(block, 128)
+
+    def part(start, size):
+        return rows_ref[:, :, start : start + size].astype(f32).reshape(clips * padded, size)
+
+    at = 2 * width
+    frame, att, head = [part(at + i * step, step)[:, :block] for i in range(3)]
+    out_out[...] = dot(att.astype(bf16), part(0, width).astype(bf16), ((0,), (0,)))
+    gloss_out[...] = dot(
+        frame.astype(bf16), part(at + 3 * step, vocab).astype(bf16), ((0,), (0,))
+    )
+    head_out[...] = jnp.sum(head, axis=0, keepdims=True)
+    gains = jnp.sum(cols_ref[:, :, lanes - 128 :].astype(f32), axis=0)
+    gain_out[...] = jnp.transpose(gains)[127:128]
     values = None
     for c in range(clips):
-        ga = by_head(ga_ref[c].astype(f32)[:frames], head_lanes).astype(bf16)
+        ga = by_head(rows_ref[c, :, width : 2 * width].astype(f32)[:frames], head_lanes).astype(bf16)
         part = dot(cols_ref[c, :, :head_lanes], ga)
         values = part if values is None else values + part
     low = low_lanes(block)
@@ -522,8 +585,7 @@
     gain_row = attn_gain.reshape(1, width)
 
     own = jnp.pad(clip_tokens[0], ((0, 0), (0, here * seq_count - patches), (0, 0)))
-    x = lax.all_to_all(own, "seq", split_axis=1, concat_axis=0, tiled=True)
-    q, k, v, probs, low, normed, inv, sums = pl.pallas_call(
+    q, k, v, probs, low, normed, inv, all_sums = pl.pallas_call(
         forward_kernel,
         out_shape=(
             shape((rows, width), bf16),
@@ -533,14 +595,22 @@
             shape((rows, width), bf16),
             shape((rows, width), f32),
             shape((rows, 128), f32),
-            shape((2, padded, width), f32),
+            shape((seq_count, 2, padded, width), f32),
         ),
-        in_specs=[VM] * 3,
+        in_specs=[VM, VM, pl.BlockSpec(memory_space=pl.ANY)],
         out_specs=(VM,) * 8,
-        compiler_params=params(),
+        scratch_shapes=[
+            pltpu.VMEM((frames, here, width), bf16),
+            pltpu.VMEM(qkv_weight.shape, bf16),
+            pltpu.SemaphoreType.DMA,
+            pltpu.SemaphoreType.DMA((2, seq_count - 1)),
+            pltpu.SemaphoreType.DMA((2, seq_count - 1)),
+        ],
+        compiler_params=pltpu.CompilerParams(
+            vmem_limit_bytes=56 << 20, collective_id=1, has_side_effects=True
+        ),
         name="forward",
-    )(x, gain_row, qkv_weight)
-    all_sums = lax.all_gather(sums, "seq", axis=0)
+    )(own, gain_row, qkv_weight)
     loss, frame_rows, gl, head_part, grad_mixed, mixed_low, ga, sum_att = pl.pallas_call(
         functools.partial(middle_kernel, patches, frames),
         out_shape=(
@@ -560,11 +630,12 @@
     )(gloss_targets, target_lengths, all_sums, out_weight, head_gain.reshape(1, width), gloss_weight)
 
     def cut(array):
-        return lax.dynamic_slice_in_dim(array, me * block, block, 1)
+        part = lax.dynamic_slice_in_dim(array, me * block, block, 1)
+        return jnp.pad(part.astype(bf16), ((0, 0), (0, up(block, 128) - block)))
 
     head8 = jnp.concatenate([head_part[:1], jnp.zeros((padded - 1, width), f32)], axis=0)
     packed = jnp.concatenate(
-        [mixed_low, ga, gl, cut(frame_rows), cut(sum_att).astype(bf16), cut(head8).astype(bf16)], axis=1
+        [mixed_low, ga, cut(frame_rows), cut(sum_att), cut(head8), gl], axis=1
     )
     gt, dw, cols = pl.pallas_call(
         functools.partial(backward_kernel, patches, frames, here),
@@ -580,7 +651,7 @@
         name="backward",
     )(q, k, v, probs, low, normed, inv, ga, grad_mixed, gain_row, qkv_weight)
     half = clips // 2
-    chunk_count = 4
+    chunk_count = min(8, block // 16)
     dw_sum, cols_all, gathered, back = pl.pallas_call(
         functools.partial(exchange_kernel, chunk_count),
         out_shape=(
@@ -602,11 +673,6 @@
     back = back.transpose(1, 0, 2, 3).reshape(local, seq_count * here, width)
     grad_tokens = back[None, :, :patches]
 
-    def part(start, size):
-        return gathered[:, :, start : start + size]
-
-    flat = clips * padded
-    at = 2 * width + vocab
     qkv_share, out_share, gloss_share, head_share, gain_share = pl.pallas_call(
         functools.partial(final_kernel, frames),
         out_shape=(
@@ -614,26 +680,17 @@
             shape((block, width), f32),
             shape((block, vocab), f32),
             shape((1, block), f32),
-            shape((block, 128), f32),
+            shape((1, block), f32),
         ),
-        in_specs=[VM] * 8,
+        in_specs=[VM] * 3,
         out_specs=(VM,) * 5,
         compiler_params=params(),
         name="final",
-    )(
-        dw_sum,
-        cols_all,
-        part(at + block, block).reshape(flat, block),
-        part(0, width).reshape(flat, width),
-        part(at, block).reshape(flat, block),
-        part(2 * width, vocab).reshape(flat, vocab),
-        part(width, width),
-        part(at + 2 * block, block).reshape(flat, block),
-    )
+    )(dw_sum, cols_all, gathered)
     return (
         loss[0, :1],
         grad_tokens,
-        gain_share[:, 127],
+        gain_share[0],
         qkv_share,
         out_share,
         head_share[0],

time: 148 us -> 134 us (0.905)
  Pallas kernels: 97.7 us -> 116 us
  local copies, waits for them, and re-layouts: 25.5 us -> 15.4 us
  blocking collectives: 6.74 us -> 0 us
  waiting for transfers between devices: 6.12 us -> 0 us
  other arithmetic: 5.27 us -> 0.77 us
  starting transfers between devices: 4.24 us -> 0 us
    pallas_call x1, Pallas kernels: 8.17 us -> 20.6 us  [per_device(): pl.pallas_call(forward_kernel, out_shape=(shape((rows, width), bf16), sha...]
    all_gather x1 -> x0, blocking collectives: 6.74 us -> none  [per_device(): all_sums = lax.all_gather(sums, 'seq', axis=0)]
    all_to_all x1 -> x0, waiting for transfers between devices: 6.12 us -> none  [per_device(): x = lax.all_to_all(own, 'seq', split_axis=1, concat_axis=0, tiled=True)]
    pallas_call x1, Pallas kernels: 65.8 us -> 71.3 us  [per_device(): pl.pallas_call(functools.partial(exchange_kernel, chunk_count), out_shape...]
    all_to_all x1 -> x0, starting transfers between devices: 4.24 us -> none  [per_device(): x = lax.all_to_all(own, 'seq', split_axis=1, concat_axis=0, tiled=True)]
    unnamed x12 -> x10, local copies, waits for them, and re-layouts: 13.9 us -> 9.9 us
    unnamed x1, other arithmetic: 4.49 us -> 0.77 us
    slice x2 -> x0, local copies, waits for them, and re-layouts: 3.33 us -> none  [the longest x1 1.68 us: part(): return gathered[:, :, start:start + size]]
  transfers between devices with their start and end apart: 1 -> 0, of which waited for: 1 -> 0; matrix products, arithmetic and copies ran while one was open for 2% -> 0% of each run, Pallas kernels for 0% -> 0%
where the time goes in v2:
time: 134 us; the launch traced here: 133 us
  Pallas kernels  116 us (87%)
  local copies, waits for them, and re-layouts  15.4 us (11%)
    pallas_call x1, Pallas kernels, per_device(): pl.pallas_call(functools.partial(exchange_kernel, chunk_count), out_shape...  71.3 us
    pallas_call x1, Pallas kernels, per_device(): pl.pallas_call(forward_kernel, out_shape=(shape((rows, width), bf16), sha...  20.6 us
    pallas_call x1, Pallas kernels, per_device(): pl.pallas_call(functools.partial(backward_kernel, patches, frames, here),...  12.1 us
    unnamed x10, local copies, waits for them, and re-layouts  9.9 us
    pallas_call x1, Pallas kernels, per_device(): pl.pallas_call(functools.partial(middle_kernel, patches, frames), out_sha...  6.78 us
    pallas_call x1, Pallas kernels, per_device(): pl.pallas_call(functools.partial(final_kernel, frames), out_shape=(shape(...  4.86 us

profile of v2, /device:TPU:0, one launch (start us, length us, event | category | flops | bytes accessed | tf_op | source)
XLA Modules:
  0.0 133.2 jit_solution(14422673263654614594)
XLA Ops:
  1.3 1.9 %pad.5.own_ref = bf16[1,256,1024]{2,1,0:T(8,128)(2,1)} pad(bf16[1,196,1024]{2,1,0:T(8,128)(2,1)} %bitcast.13, bf16[]{:T(256)} %constant.3.clone.1), padding=0_0x0_60x0_0 | pad | bytes 925698 | tf_op jit(solution)/shard_map/jit(_pad)/pad | solution.py:587
  3.1 4.3 %copy.15.wg_ref = bf16[1024,1200]{1,0:T(8,128)(2,1)} copy(bf16[1024,1200]{0,1:T(8,128)(2,1)} %param.13) | data formatting | bytes 4915200 | tf_op args[5]
  7.5 20.6 %forward.1 = (bf16[256,1024]{1,0:T(8,128)(2,1)}, bf16[256,1024]{1,0:T(8,128)(2,1)}, bf16[256,1024]{1,0:T(8,128)(2,1)}, f32[256,128]{1,0:T(8,128)}, bf16[256,1024...) custom-call(bf16[1,256,1024]{2,1,0:T(8,128)(2,1)} %pad.5.own_ref, ...), custom_call_target="tpu_custom_call" | custom-call | tf_op jit(solution)/shard_map/forward/pallas_call | solution.py:588
  28.1 0.0 copy-start.1
  28.1 6.8 %middle.1 = (f32[8,128]{1,0:T(8,128)}, bf16[8,1024]{1,0:T(8,128)(2,1)}, bf16[8,1200]{1,0:T(8,128)(2,1)}, f32[8,1024]{1,0:T(8,128)}, f32[8,1024]{1,0:T(8,128)}, /...) custom-call(s32[1,2]{1,0:T(1,128)} %labels_ref.1, s32[1]{0:T(128)S(6)} %copy.22.length_ref, ...), custom_call_target="tpu_custom_call" | custom-call | tf_op jit(solution)/shard_map/middle/pallas_call | solution.py:614
  34.9 1.2 slice.8
  36.1 0.7 constant_dynamic-update-slice_fusion.5
  36.8 0.7 constant_dynamic-update-slice_fusion.4
  37.5 0.7 constant_dynamic-update-slice_fusion.3
  38.2 0.7 constant_dynamic-update-slice_fusion.2
  38.9 0.0 copy-done.1
  38.9 0.8 constant_dynamic-update-slice_fusion.1
  39.7 0.7 constant_dynamic-update-slice_fusion.rows_ref
  40.4 0.0 copy-start
  40.4 12.1 %backward.1 = (bf16[4,64,1024]{2,1,0:T(8,128)(2,1)}, bf16[1024,2048]{1,0:T(8,128)(2,1)}, bf16[1024,128]{1,0:T(8,128)(2,1)}) custom-call(bf16[256,1024]{1,0:T(8,128)(2,1)} %get-tuple-element.37.q_ref, bf16[256,1024]{1,0:T(8,128)(2,1)} %get-tuple-element.38.k_ref, bf16[256,1024]{1,0:T(8,128)(2,1)} %get-tuple-element.39.v_ref, ...), custom_call_target="tpu_custom_call" | custom-call | tf_op jit(solution)/shard_map/backward/pallas_call | solution.py:640
  52.5 0.0 copy-done
  52.5 71.3 %exchange.1 = (bf16[256,2048]{1,0:T(8,128)(2,1)}, bf16[2,4,256,128]{3,2,1,0:T(8,128)(2,1)}, bf16[2,4,8,4016]{3,2,1,0:T(8,128)(2,1)}, bf16[4,1,64,1024]{3,2,1,0:T(8,128)(2,1)}) custom-call(bf16[1024,2048]{1,0:T(8,128)(2,1)} %get-tuple-element.46.dw_ref, bf16[1024,128]{1,0:T(8,128)(2,1)} %get-tuple-element.47.cols_ref, bf16[8,4016]{1,0:T(8,128)(2,1)} %copy-done, ...), custom_call_target="tpu_custom_call" | custom-call | tf_op jit(solution)/shard_map/exchange/pallas_call | solution.py:655
  123.8 1.8 %slice_bitcast_fusion = bf16[1,1,196,1024]{3,2,1,0:T(8,128)(2,1)} fusion(bf16[1,256,1024]{2,1,0:T(8,128)(2,1)} %bitcast.14), kind=kLoop, calls=%fused_computation | loop fusion | bytes 802816 | tf_op jit(solution)/shard_map/broadcast_in_dim | solution.py:674
  125.6 4.9 %final.1 = (f32[256,3072]{1,0:T(8,128)}, f32[256,1024]{1,0:T(8,128)}, f32[256,1200]{1,0:T(8,128)}, f32[1,256]{1,0:T(1,128)}, f32[1,256]{1,0:T(1,128)}) custom-call(bf16[256,2048]{1,0:T(8,128)(2,1)} %get-tuple-element.55.qk_ref, bf16[8,256,128]{2,1,0:T(8,128)(2,1)} %bitcast.11, bf16[8,8,4016]{2,1,0:T(8,128)(2,1)} %bitcast.12), custom_call_target="tpu_custom_call" | custom-call | tf_op jit(solution)/shard_map/final/pallas_call | solution.py:676
  130.5 2.7 %copy.16 = f32[256,1200]{0,1:T(8,128)} copy(f32[256,1200]{1,0:T(8,128)} %get-tuple-element.69) | data formatting | bytes 2457600
Async XLA Ops:
  28.1 10.8 %copy-start.1 = (pred[8]{0:T(512)(128)(4,1)S(1)}, pred[8]{0:T(512)(128)(4,1)}, u32[]{:S(2)}) copy-start(pred[8]{0:T(512)(128)(4,1)} %constant.14.clone.1) | copy-start | bytes 28
  40.4 12.1 %copy-start = (bf16[8,4016]{1,0:T(8,128)(2,1)}, bf16[8,4016]{1,0:T(8,128)(2,1)S(1)}, u32[]{:S(2)}) copy-start(bf16[8,4016]{1,0:T(8,128)(2,1)S(1)} %constant_dynamic-update-slice_fusion.rows_ref) | copy-start | bytes 192772

commit v3 on v2

--- a/solution.py
+++ b/solution.py
@@ -147,11 +147,14 @@
 
 def middle_kernel(
     patches, frames, labels_ref, length_ref, sums_ref, wo_ref, gain_ref, wg_ref,
-    loss_ref, frame_ref, gl_ref, head_ref, mix_ref, low_ref, ga_ref, att_ref,
+    loss_ref, packed_ref, mix_ref, ga_ref, wide_ref,
 ):
+    width = wo_ref.shape[0]
+    block = width // sums_ref.shape[0]
+    step = up(block, 128)
     total = jnp.sum(sums_ref[...], axis=0)
     sum_tok, sum_att = total[0], total[1]
-    att_ref[...] = sum_att
+    wide_ref[1] = sum_att
     hi = sum_att.astype(bf16)
     lo = (sum_att - hi.astype(f32)).astype(bf16)
     pooled = (sum_tok + dot(hi, wo_ref[...]) + dot(lo, wo_ref[...])) * (1.0 / patches)
@@ -159,8 +162,8 @@
     inv = lax.rsqrt(jnp.mean(centred * centred, axis=1, keepdims=True) + epsilon)
     plain = centred * inv
     frame = (plain * gain_ref[...]).astype(bf16)
-    frame_ref[...] = frame
-    logits = dot(frame, wg_ref[...])
+    wide_ref[0] = frame.astype(f32)
+    logits = dot(frame, wg_ref[...], ((1,), (1,)))
     padded, vocab = logits.shape
     raised = jnp.exp(logits)
     denom = jnp.sum(raised, axis=1, keepdims=True)
@@ -218,9 +221,17 @@
         d_logs = d_logs + jnp.where(gloss == labels_ref[0, i], part, 0.0)
     d_logits = d_logs - soft * jnp.sum(emit_grad, axis=1, keepdims=True)
     gl = d_logits.astype(bf16)
-    gl_ref[...] = gl
-    grad_frame = dot(gl, wg_ref[...], ((1,), (1,)))
-    head_ref[...] = jnp.broadcast_to(jnp.sum(grad_frame * plain, axis=0, keepdims=True), head_ref.shape)
+    packed_ref[:, 2 * width + 3 * step :] = gl
+    grad_frame = dot(gl, wg_ref[...])
+    head = jnp.sum(grad_frame * plain, axis=0, keepdims=True)
+    first_row = lax.broadcasted_iota(jnp.int32, (padded, width), 0) == 0
+    wide_ref[2] = jnp.where(first_row, jnp.broadcast_to(head, (padded, width)), 0.0)
+    start_at = lax.axis_index("seq") * block
+    for i in range(3):
+        part = wide_ref[i, :, pl.ds(pl.multiple_of(start_at // 128 * 128, 128), step)]
+        for shift in range(block, 128, block):
+            part = jnp.where(lax.rem(start_at, 128) == shift, pltpu.roll(part, 128 - shift, 1), part)
+        packed_ref[:, 2 * width + i * step : 2 * width + (i + 1) * step] = part.astype(bf16)
     scaled = grad_frame * gain_ref[...]
     grad_pooled = inv * (
         scaled
@@ -230,8 +241,10 @@
     grad_mixed = grad_pooled * (1.0 / patches)
     mix_ref[...] = grad_mixed
     mixed_low = grad_mixed.astype(bf16)
-    low_ref[...] = mixed_low
-    ga_ref[...] = dot(mixed_low, wo_ref[...], ((1,), (1,))).astype(bf16)
+    packed_ref[:, :width] = mixed_low
+    ga = dot(mixed_low, wo_ref[...], ((1,), (1,))).astype(bf16)
+    ga_ref[...] = ga
+    packed_ref[:, width : 2 * width] = ga
 
 
 def backward_kernel(
@@ -311,7 +324,7 @@
     clips, block, lanes = cols_ref.shape
     head_lanes = up(frames * H, 128)
     padded = rows_ref.shape[1]
-    width, vocab = out_out.shape[1], gloss_out.shape[1]
+    width, vocab = out_out.shape[1], gloss_out.shape[0]
     step = up(block, 128)
 
     def part(start, size):
@@ -321,7 +334,7 @@
     frame, att, head = [part(at + i * step, step)[:, :block] for i in range(3)]
     out_out[...] = dot(att.astype(bf16), part(0, width).astype(bf16), ((0,), (0,)))
     gloss_out[...] = dot(
-        frame.astype(bf16), part(at + 3 * step, vocab).astype(bf16), ((0,), (0,))
+        part(at + 3 * step, vocab).astype(bf16), frame.astype(bf16), ((0,), (0,))
     )
     head_out[...] = jnp.sum(head, axis=0, keepdims=True)
     gains = jnp.sum(cols_ref[:, :, lanes - 128 :].astype(f32), axis=0)
@@ -611,32 +624,21 @@
         ),
         name="forward",
     )(own, gain_row, qkv_weight)
-    loss, frame_rows, gl, head_part, grad_mixed, mixed_low, ga, sum_att = pl.pallas_call(
+    loss, packed, grad_mixed, ga = pl.pallas_call(
         functools.partial(middle_kernel, patches, frames),
         out_shape=(
             shape((8, 128), f32),
-            shape((padded, width), bf16),
-            shape((padded, vocab), bf16),
-            shape((8, width), f32),
+            shape((padded, 2 * width + 3 * up(block, 128) + vocab), bf16),
             shape((padded, width), f32),
             shape((padded, width), bf16),
-            shape((padded, width), bf16),
-            shape((padded, width), f32),
         ),
         in_specs=[SM, SM] + [VM] * 4,
-        out_specs=(VM,) * 8,
+        out_specs=(VM,) * 4,
+        scratch_shapes=[pltpu.VMEM((3, padded, width), f32)],
         compiler_params=params(),
         name="middle",
-    )(gloss_targets, target_lengths, all_sums, out_weight, head_gain.reshape(1, width), gloss_weight)
-
-    def cut(array):
-        part = lax.dynamic_slice_in_dim(array, me * block, block, 1)
-        return jnp.pad(part.astype(bf16), ((0, 0), (0, up(block, 128) - block)))
-
-    head8 = jnp.concatenate([head_part[:1], jnp.zeros((padded - 1, width), f32)], axis=0)
-    packed = jnp.concatenate(
-        [mixed_low, ga, cut(frame_rows), cut(sum_att), cut(head8), gl], axis=1
-    )
+    )(gloss_targets, target_lengths, all_sums, out_weight, head_gain.reshape(1, width), gloss_weight.T)
+
     gt, dw, cols = pl.pallas_call(
         functools.partial(backward_kernel, patches, frames, here),
         out_shape=(
@@ -651,7 +653,7 @@
         name="backward",
     )(q, k, v, probs, low, normed, inv, ga, grad_mixed, gain_row, qkv_weight)
     half = clips // 2
-    chunk_count = min(8, block // 16)
+    chunk_count = 4
     dw_sum, cols_all, gathered, back = pl.pallas_call(
         functools.partial(exchange_kernel, chunk_count),
         out_shape=(
@@ -678,7 +680,7 @@
         out_shape=(
             shape((block, 3 * width), f32),
             shape((block, width), f32),
-            shape((block, vocab), f32),
+            shape((vocab, block), f32),
             shape((1, block), f32),
             shape((1, block), f32),
         ),
@@ -694,7 +696,7 @@
         qkv_share,
         out_share,
         head_share[0],
-        gloss_share,
+        gloss_share.T,
     )
 
 

time: 134 us -> 114 us (0.85)
  local copies, waits for them, and re-layouts: 15.4 us -> 4.83 us
  Pallas kernels: 116 us -> 108 us
    unnamed x10 -> x0, local copies, waits for them, and re-layouts: 9.9 us -> none
    pallas_call x1, Pallas kernels: 71.3 us -> 63.6 us  [per_device(): pl.pallas_call(functools.partial(exchange_kernel, chunk_count), out_shape...]
where the time goes in v3:
time: 114 us
  Pallas kernels  108 us (95%)
  local copies, waits for them, and re-layouts  4.83 us (4%)
  between operations  1.3 us (1%)
    pallas_call x1, Pallas kernels, per_device(): pl.pallas_call(functools.partial(exchange_kernel, chunk_count), out_shape...  63.6 us
    pallas_call x1, Pallas kernels, per_device(): pl.pallas_call(forward_kernel, out_shape=(shape((rows, width), bf16), sha...  20.6 us
    pallas_call x1, Pallas kernels, per_device(): pl.pallas_call(functools.partial(backward_kernel, patches, frames, here),...  12.1 us
    pallas_call x1, Pallas kernels, per_device(): pl.pallas_call(functools.partial(middle_kernel, patches, frames), out_sha...  6.88 us
    pallas_call x1, Pallas kernels, per_device(): pl.pallas_call(functools.partial(final_kernel, frames), out_shape=(shape(...  4.81 us

profile of v3, /device:TPU:0, one launch (start us, length us, event | category | flops | bytes accessed | tf_op | source)
XLA Modules:
  0.0 114.1 jit_solution(1192258728513770293)
XLA Ops:
  1.3 1.9 %pad.4.own_ref = bf16[1,256,1024]{2,1,0:T(8,128)(2,1)} pad(bf16[1,196,1024]{2,1,0:T(8,128)(2,1)} %bitcast.16, bf16[]{:T(256)} %constant.2.clone.1), padding=0_0x0_60x0_0 | pad | bytes 925698 | tf_op jit(solution)/shard_map/jit(_pad)/pad | solution.py:600
  3.1 20.6 %forward.1 = (bf16[256,1024]{1,0:T(8,128)(2,1)}, bf16[256,1024]{1,0:T(8,128)(2,1)}, bf16[256,1024]{1,0:T(8,128)(2,1)}, f32[256,128]{1,0:T(8,128)}, bf16[256,1024...) custom-call(bf16[1,256,1024]{2,1,0:T(8,128)(2,1)} %pad.4.own_ref, ...), custom_call_target="tpu_custom_call" | custom-call | tf_op jit(solution)/shard_map/forward/pallas_call | solution.py:601
  23.8 6.9 %middle.1 = (f32[8,128]{1,0:T(8,128)}, bf16[8,4016]{1,0:T(8,128)(2,1)}, f32[8,1024]{1,0:T(8,128)}, bf16[8,1024]{1,0:T(8,128)(2,1)}) custom-call(s32[1,2]{1,0:T(1,128)} %labels_ref.1, s32[1]{0:T(128)S(6)} %copy.15.length_ref, f32[4,2,8,1024]{3,2,1,0:T(8,128)} %get-tuple-element.31.sums_ref, bf16[1024,1024]{1,0:T(8,128)(2,1)} %wo_ref.1, f32[1,1024]{1,0:T(1,128)} %bitcast.20, ...), custom_call_target="tpu_custom_call" | custom-call | tf_op jit(solution)/shard_map/middle/pallas_call | solution.py:627
  30.7 1.2 %slice.6 = f32[1,1]{1,0:T(1,128)} slice(f32[8,128]{1,0:T(8,128)} %get-tuple-element.32), slice={[0:1], [0:1]} | slice | bytes 8 | tf_op jit(solution)/shard_map/slice | solution.py:693
  31.9 12.1 %backward.1 = (bf16[4,64,1024]{2,1,0:T(8,128)(2,1)}, bf16[1024,2048]{1,0:T(8,128)(2,1)}, bf16[1024,128]{1,0:T(8,128)(2,1)}) custom-call(bf16[256,1024]{1,0:T(8,128)(2,1)} %get-tuple-element.33.q_ref, bf16[256,1024]{1,0:T(8,128)(2,1)} %get-tuple-element.34.k_ref, bf16[256,1024]{1,0:T(8,128)(2,1)} %get-tuple-element.35.v_ref, ...), custom_call_target="tpu_custom_call" | custom-call | tf_op jit(solution)/shard_map/backward/pallas_call | solution.py:642
  43.9 63.6 %exchange.1 = (bf16[256,2048]{1,0:T(8,128)(2,1)}, bf16[2,4,256,128]{3,2,1,0:T(8,128)(2,1)}, bf16[2,4,8,4016]{3,2,1,0:T(8,128)(2,1)}, bf16[4,1,64,1024]{3,2,1,0:T(8,128)(2,1)}) custom-call(bf16[1024,2048]{1,0:T(8,128)(2,1)} %get-tuple-element.42.dw_ref, bf16[1024,128]{1,0:T(8,128)(2,1)} %get-tuple-element.43.cols_ref, ...), custom_call_target="tpu_custom_call" | custom-call | tf_op jit(solution)/shard_map/exchange/pallas_call | solution.py:657
  107.5 1.8 %slice_bitcast_fusion = bf16[1,1,196,1024]{3,2,1,0:T(8,128)(2,1)} fusion(bf16[1,256,1024]{2,1,0:T(8,128)(2,1)} %bitcast.17), kind=kLoop, calls=%fused_computation | loop fusion | bytes 802816 | tf_op jit(solution)/shard_map/broadcast_in_dim | solution.py:676
  109.3 4.8 %final.1 = (f32[256,3072]{1,0:T(8,128)}, f32[256,1024]{1,0:T(8,128)}, f32[1200,256]{1,0:T(8,128)}, f32[1,256]{1,0:T(1,128)}, f32[1,256]{1,0:T(1,128)}) custom-call(bf16[256,2048]{1,0:T(8,128)(2,1)} %get-tuple-element.47.qk_ref, bf16[8,256,128]{2,1,0:T(8,128)(2,1)} %bitcast.14, bf16[8,8,4016]{2,1,0:T(8,128)(2,1)} %bitcast.15), custom_call_target="tpu_custom_call" | custom-call | tf_op jit(solution)/shard_map/final/pallas_call | solution.py:678

commit v4 on v3

--- a/solution.py
+++ b/solution.py
@@ -542,6 +542,8 @@
     stages = [first, second, third, fourth, fifth, sixth, seventh]
     for c in range(chunk_count):
         first(c)
+    for c in range(chunk_count):
+        second(c)
     all_rows_ref[x, z] = rows_ref[...]
     row_waits = [
         send(rows_ref, all_rows_ref.at[x, z], row_sem, (step - 1,), z_peer(step))
@@ -554,11 +556,11 @@
             send(gt_ref.at[pl.ds(to * local, local)], back_ref.at[me], token_sem, (step - 1,), at(clip, to))
         )
     back_ref[me] = gt_ref[pl.ds(me * local, local)]
-    for wave in range(1, chunk_count + len(stages) - 1):
+    for wave in range(2, chunk_count + len(stages) - 1):
         for c in range(chunk_count):
-            if 1 <= wave - c < len(stages):
+            if 2 <= wave - c < len(stages):
                 stages[wave - c](c)
-        if wave == 2:
+        if wave == 3:
             for copy in row_waits:
                 copy.wait_recv()
             row_waits = [send(all_rows_ref.at[x], all_rows_ref.at[x], row_sem, (half - 1,), x_peer)]

time: 114 us -> 110 us (0.965)
  Pallas kernels: 108 us -> 104 us
    pallas_call x1, Pallas kernels: 63.6 us -> 59.3 us  [per_device(): pl.pallas_call(functools.partial(exchange_kernel, chunk_count), out_shape...]
where the time goes in v4:
time: 110 us
  Pallas kernels  104 us (95%)
  local copies, waits for them, and re-layouts  4.83 us (4%)
  between operations  1.3 us (1%)
    pallas_call x1, Pallas kernels, per_device(): pl.pallas_call(functools.partial(exchange_kernel, chunk_count), out_shape...  59.3 us
    pallas_call x1, Pallas kernels, per_device(): pl.pallas_call(forward_kernel, out_shape=(shape((rows, width), bf16), sha...  20.6 us
    pallas_call x1, Pallas kernels, per_device(): pl.pallas_call(functools.partial(backward_kernel, patches, frames, here),...  12.1 us
    pallas_call x1, Pallas kernels, per_device(): pl.pallas_call(functools.partial(middle_kernel, patches, frames), out_sha...  6.88 us
    pallas_call x1, Pallas kernels, per_device(): pl.pallas_call(functools.partial(final_kernel, frames), out_shape=(shape(...  4.81 us

profile of v4, /device:TPU:0, one launch (start us, length us, event | category | flops | bytes accessed | tf_op | source)
XLA Modules:
  0.0 109.8 jit_solution(9204626149695206434)
XLA Ops:
  1.3 1.9 %pad.4.own_ref = bf16[1,256,1024]{2,1,0:T(8,128)(2,1)} pad(bf16[1,196,1024]{2,1,0:T(8,128)(2,1)} %bitcast.16, bf16[]{:T(256)} %constant.2.clone.1), padding=0_0x0_60x0_0 | pad | bytes 925698 | tf_op jit(solution)/shard_map/jit(_pad)/pad | solution.py:602
  3.1 20.6 %forward.1 = (bf16[256,1024]{1,0:T(8,128)(2,1)}, bf16[256,1024]{1,0:T(8,128)(2,1)}, bf16[256,1024]{1,0:T(8,128)(2,1)}, f32[256,128]{1,0:T(8,128)}, bf16[256,1024...) custom-call(bf16[1,256,1024]{2,1,0:T(8,128)(2,1)} %pad.4.own_ref, ...), custom_call_target="tpu_custom_call" | custom-call | tf_op jit(solution)/shard_map/forward/pallas_call | solution.py:603
  23.8 6.9 %middle.1 = (f32[8,128]{1,0:T(8,128)}, bf16[8,4016]{1,0:T(8,128)(2,1)}, f32[8,1024]{1,0:T(8,128)}, bf16[8,1024]{1,0:T(8,128)(2,1)}) custom-call(s32[1,2]{1,0:T(1,128)} %labels_ref.1, s32[1]{0:T(128)S(6)} %copy.15.length_ref, f32[4,2,8,1024]{3,2,1,0:T(8,128)} %get-tuple-element.31.sums_ref, bf16[1024,1024]{1,0:T(8,128)(2,1)} %wo_ref.1, f32[1,1024]{1,0:T(1,128)} %bitcast.20, ...), custom_call_target="tpu_custom_call" | custom-call | tf_op jit(solution)/shard_map/middle/pallas_call | solution.py:629
  30.7 1.2 %slice.6 = f32[1,1]{1,0:T(1,128)} slice(f32[8,128]{1,0:T(8,128)} %get-tuple-element.32), slice={[0:1], [0:1]} | slice | bytes 8 | tf_op jit(solution)/shard_map/slice | solution.py:695
  31.9 12.1 %backward.1 = (bf16[4,64,1024]{2,1,0:T(8,128)(2,1)}, bf16[1024,2048]{1,0:T(8,128)(2,1)}, bf16[1024,128]{1,0:T(8,128)(2,1)}) custom-call(bf16[256,1024]{1,0:T(8,128)(2,1)} %get-tuple-element.33.q_ref, bf16[256,1024]{1,0:T(8,128)(2,1)} %get-tuple-element.34.k_ref, bf16[256,1024]{1,0:T(8,128)(2,1)} %get-tuple-element.35.v_ref, ...), custom_call_target="tpu_custom_call" | custom-call | tf_op jit(solution)/shard_map/backward/pallas_call | solution.py:644
  43.9 59.3 %exchange.1 = (bf16[256,2048]{1,0:T(8,128)(2,1)}, bf16[2,4,256,128]{3,2,1,0:T(8,128)(2,1)}, bf16[2,4,8,4016]{3,2,1,0:T(8,128)(2,1)}, bf16[4,1,64,1024]{3,2,1,0:T(8,128)(2,1)}) custom-call(bf16[1024,2048]{1,0:T(8,128)(2,1)} %get-tuple-element.42.dw_ref, bf16[1024,128]{1,0:T(8,128)(2,1)} %get-tuple-element.43.cols_ref, ...), custom_call_target="tpu_custom_call" | custom-call | tf_op jit(solution)/shard_map/exchange/pallas_call | solution.py:659
  103.2 1.8 %slice_bitcast_fusion = bf16[1,1,196,1024]{3,2,1,0:T(8,128)(2,1)} fusion(bf16[1,256,1024]{2,1,0:T(8,128)(2,1)} %bitcast.17), kind=kLoop, calls=%fused_computation | loop fusion | bytes 802816 | tf_op jit(solution)/shard_map/broadcast_in_dim | solution.py:678
  105.0 4.8 %final.1 = (f32[256,3072]{1,0:T(8,128)}, f32[256,1024]{1,0:T(8,128)}, f32[1200,256]{1,0:T(8,128)}, f32[1,256]{1,0:T(1,128)}, f32[1,256]{1,0:T(1,128)}) custom-call(bf16[256,2048]{1,0:T(8,128)(2,1)} %get-tuple-element.47.qk_ref, bf16[8,256,128]{2,1,0:T(8,128)(2,1)} %bitcast.14, bf16[8,8,4016]{2,1,0:T(8,128)(2,1)} %bitcast.15), custom_call_target="tpu_custom_call" | custom-call | tf_op jit(solution)/shard_map/final/pallas_call | solution.py:680
